TPU v7x, 32 devices: a whole 2x2x4 slice. The times are simulated.
32 devices in a mesh: dp: 8 (over y, x, core), tensor: 4 (over z).
Axes of the slice: x: 2, y: 2, z: 4, core: 2. Of those that a mesh axis runs over, the one named last changes fastest.
Arguments:
- inputs: float32 [8192, 1024], P('dp', 'tensor'), may hold values from -6 to 6
- norm_in: float32 [1024], replicated, may hold values from 0.5 to 1.5
- w_value: bfloat16 [1024, 2048], P(None, 'tensor'), may hold values from -0.1875 to 0.1875
- expand: float32 [1024, 16], P('tensor'), may hold values from -4 to 4
- ema_rate: float32 [1024, 16], P('tensor'), may hold values from 0.02 to 0.9
- damping: float32 [1024, 16], P('tensor'), may hold values from 0.3 to 1
- project: float32 [1024, 16], P('tensor'), may hold values from -1.5 to 1.5
- ema_skip: float32 [1024], P('tensor'), may hold values from -4 to 4
- w_shared: bfloat16 [1024, 128], P('tensor'), may hold values from -0.1875 to 0.1875
- qk_affine: float32 [3, 128], replicated, may hold values from -6 to 6
- w_reset: bfloat16 [1024, 2048], P('tensor'), may hold values from -0.1875 to 0.1875
- w_update: bfloat16 [1024, 1024], P('tensor'), may hold values from -0.1875 to 0.1875
- w_hidden: bfloat16 [1024, 1024], P('tensor'), may hold values from -0.1875 to 0.1875
- u_hidden: bfloat16 [2048, 1024], P('tensor'), may hold values from -0.375 to 0.375
- norm_out: float32 [1024], replicated, may hold values from 0.5 to 1.5
- w_in: bfloat16 [1024, 4096], P(None, 'tensor'), may hold values from -0.1875 to 0.1875
- w_out: bfloat16 [4096, 1024], P('tensor'), may hold values from -0.09375 to 0.09375
- cotangent: float32 [8192, 1024], P('dp', 'tensor'), may hold values from -6 to 6
- piece_starts: int32 [8, 2], P('dp'), may hold values from 0 to 768, as said below
Outputs:
- outputs: float32 [8192, 1024], P('dp', 'tensor')
- grad_inputs: float32 [8192, 1024], P('dp', 'tensor')
- grad_norm_in: float32 [1024], P('tensor')
- grad_w_value: float32 [1024, 2048], P('dp', 'tensor')
- grad_expand: float32 [1024, 16], P('tensor')
- grad_ema_rate: float32 [1024, 16], P('tensor')
- grad_damping: float32 [1024, 16], P('tensor')
- grad_project: float32 [1024, 16], P('tensor')
- grad_ema_skip: float32 [1024], P('tensor')
- grad_w_shared: float32 [1024, 128], P('tensor', 'dp')
- grad_qk_affine: float32 [3, 128], replicated
- grad_w_reset: float32 [1024, 2048], P('tensor', 'dp')
- grad_w_update: float32 [1024, 1024], P('tensor', 'dp')
- grad_w_hidden: float32 [1024, 1024], P('tensor', 'dp')
- grad_u_hidden: float32 [2048, 1024], P('tensor', 'dp')
- grad_norm_out: float32 [1024], P('tensor')
- grad_w_in: float32 [1024, 4096], P('dp', 'tensor')
- grad_w_out: float32 [4096, 1024], P('tensor', 'dp')
Inputs may be any that keep to these rules, and one draw needn't show every extreme that they name: `piece_starts`: in each sequence the 2 picture pieces of 256 tokens start at these offsets, in rising order and without intersection; all other tokens are text. The first sequence's first piece starts at token 0 and the last sequence's last piece ends at the sequence's end.
All inputs are finite; a program needn't handle non-finite values.
Results may differ from a plain program's by a relative error of at most 0.018.
Values may be sent and summed in bfloat16 or wider, within the bound.
No kernel may reach another device: no remote copies, remote signals or barrier semaphores. Data moves between devices by JAX's collectives and lax.ppermute only.
A program may use at most 192 MiB of HBM per device.

v0:
```python
from functools import partial

import jax
import jax.numpy as jnp
from jax import lax
from jax.sharding import PartitionSpec as P

PIECE = 256
QBLOCK = 512
EMA_BLOCK = 64


epsilon = 1e-05
highest = lax.Precision.HIGHEST


def toeplitz_table(kernel):
    block_size = kernel.shape[0]
    rows = jnp.arange(block_size, dtype=jnp.int32)
    lag = rows[:, None] - rows[None, :]
    picked = jnp.take(kernel, jnp.maximum(lag, 0), axis=0)
    return jnp.where((lag >= 0)[:, :, None], picked, jnp.zeros_like(picked))


def ema_mix(signal, expand, ema_rate, damping, project, ema_skip):
    length = signal.shape[0]
    channels = signal.shape[1]
    block_size = EMA_BLOCK
    decays = 1.0 - ema_rate * damping
    log_decay = jnp.log(decays)
    step_index = jnp.arange(block_size).astype(jnp.float32)
    powers = jnp.exp(step_index[:, None, None] * log_decay[None, :, :])
    inject = ema_rate * expand
    kernel = jnp.sum(powers * (project * inject)[None, :, :], axis=2)
    toeplitz = toeplitz_table(kernel)
    blocks = signal.reshape(length // block_size, block_size, channels)
    in_block = jnp.einsum("ijc,njc->nic", toeplitz, blocks, precision=highest)
    driving = jnp.einsum(
        "jch,njc->nch", powers[::-1] * inject[None, :, :], blocks, precision=highest
    )
    block_decay = jnp.exp(block_size * log_decay)

    def advance(carried, pushed):
        return (block_decay * carried + pushed, carried)

    unused, before = lax.scan(advance, jnp.zeros_like(decays), driving)
    from_before = jnp.einsum(
        "ich,nch->nic", powers * (decays * project)[None, :, :], before, precision=highest
    )
    mixed_sum = (in_block + from_before).reshape(length, channels)
    return jax.nn.silu(mixed_sum + ema_skip * signal)


def normalize_keep(values):
    centered = values - jnp.mean(values, axis=1, keepdims=True)
    inv_scale = lax.rsqrt(jnp.mean(centered * centered, axis=1, keepdims=True) + epsilon)
    return (centered * inv_scale, inv_scale)


def silu_grad(values):
    sigmoid_of = jax.nn.sigmoid(values)
    return sigmoid_of * (1.0 + values * (1.0 - sigmoid_of))


def piece_ids_of(starts, length):
    positions = jnp.arange(length, dtype=jnp.int32)
    inside = (positions[:, None] >= starts[None, :]) & (
        positions[:, None] < starts[None, :] + PIECE
    )
    labels = jnp.arange(1, starts.shape[0] + 1, dtype=jnp.int32)
    return jnp.sum(jnp.where(inside, labels[None, :], 0), axis=1)


def allowed_keys(row_pos, row_ids, piece_ids):
    key_pos = jnp.arange(piece_ids.shape[0], dtype=jnp.int32)
    causal = key_pos[None, :] <= row_pos[:, None]
    same_piece = (row_ids[:, None] == piece_ids[None, :]) & (row_ids[:, None] > 0)
    return causal | same_piece


def block_scores(queries, keys_low, piece_ids, block_index, block_rows):
    first_row = block_index * block_rows
    query_rows = lax.dynamic_slice_in_dim(queries, first_row, block_rows, 0)
    row_pos = first_row + jnp.arange(block_rows, dtype=jnp.int32)
    row_ids = lax.dynamic_slice_in_dim(piece_ids, first_row, block_rows, 0)
    scores = jnp.einsum("qz,kz->qk", query_rows, keys_low, preferred_element_type=jnp.float32)
    scores = scores * queries.shape[1] ** (-0.5)
    return (jnp.where(allowed_keys(row_pos, row_ids, piece_ids), scores, -1e30), query_rows)


def attend_forward(sequence_item):
    queries, keys_low, values, piece_ids = sequence_item
    length = queries.shape[0]
    block_rows = min(QBLOCK, length)

    def one_block(block_index):
        scores, query_rows = block_scores(queries, keys_low, piece_ids, block_index, block_rows)
        row_max = jnp.max(scores, axis=1, keepdims=True)
        exponent = jnp.exp(scores - row_max)
        row_total = jnp.sum(exponent, axis=1, keepdims=True)
        weights = (exponent / row_total).astype(jnp.bfloat16)
        attended = jnp.dot(weights, values, preferred_element_type=jnp.float32)
        return (attended, (row_max + jnp.log(row_total))[:, 0])

    attended, log_total = lax.map(one_block, jnp.arange(length // block_rows, dtype=jnp.int32))
    return (attended.reshape(length, values.shape[1]), log_total.reshape(length))


def attend_backward(sequence_item):
    queries, keys_low, values, piece_ids, log_total, grad_attended = sequence_item
    length = queries.shape[0]
    block_rows = min(QBLOCK, length)
    score_scale = queries.shape[1] ** (-0.5)
    keys_wide = keys_low.astype(jnp.float32)

    def one_block(carried, block_index):
        key_grad, value_grad = carried
        scores, query_rows = block_scores(queries, keys_low, piece_ids, block_index, block_rows)
        first_row = block_index * block_rows
        row_lse = lax.dynamic_slice_in_dim(log_total, first_row, block_rows, 0)
        grad_rows = lax.dynamic_slice_in_dim(grad_attended, first_row, block_rows, 0)
        weights = jnp.exp(scores - row_lse[:, None])
        grad_weights = jnp.einsum(
            "qv,kv->qk", grad_rows, values, preferred_element_type=jnp.float32
        )
        center = jnp.sum(weights * grad_weights, axis=1, keepdims=True)
        grad_scores = weights * (grad_weights - center) * score_scale
        query_grad = jnp.dot(
            grad_scores, keys_wide, precision=highest, preferred_element_type=jnp.float32
        )
        key_grad = key_grad + jnp.einsum(
            "qk,qz->kz",
            grad_scores,
            query_rows.astype(jnp.float32),
            precision=highest,
            preferred_element_type=jnp.float32,
        )
        value_grad = value_grad + jnp.einsum(
            "qk,qv->kv", weights.astype(jnp.bfloat16), grad_rows, preferred_element_type=jnp.float32
        )
        return ((key_grad, value_grad), query_grad)

    zeros_start = (jnp.zeros(keys_low.shape, jnp.float32), jnp.zeros(values.shape, jnp.float32))
    (key_grad, value_grad), query_grad = lax.scan(
        one_block, zeros_start, jnp.arange(length // block_rows, dtype=jnp.int32)
    )
    return (query_grad.reshape(length, queries.shape[1]), key_grad, value_grad)


def on_device(
    inputs,
    norm_in,
    w_value,
    expand,
    ema_rate,
    damping,
    project,
    ema_skip,
    w_shared,
    qk_affine,
    w_reset,
    w_update,
    w_hidden,
    u_hidden,
    norm_out,
    w_in,
    w_out,
    cotangent,
    piece_starts,
):
    tensor_rank = lax.axis_index("tensor")
    tensor_count = lax.axis_size("tensor")
    seq_count = piece_starts.shape[0]
    row_count = inputs.shape[0]
    length = row_count // seq_count
    own_width = inputs.shape[1]
    own_first = tensor_rank * own_width
    value_width = w_value.shape[1]
    shared_width = w_shared.shape[1]
    full_in = lax.all_gather(inputs, "tensor", axis=1, tiled=True)
    unit_in, inv_in = normalize_keep(full_in)
    normed = unit_in * norm_in
    normed_low = normed.astype(jnp.bfloat16)
    value_pre = jnp.dot(normed_low, w_value, preferred_element_type=jnp.float32)
    values_low = jax.nn.silu(value_pre).astype(jnp.bfloat16)
    normed_own = lax.dynamic_slice_in_dim(normed, own_first, own_width, 1)

    def mixer_rows(signal, expand_in, rate_in, damping_in, project_in, skip_in):
        per_sequence = jax.vmap(ema_mix, in_axes=(0, None, None, None, None, None))
        mixed_rows = per_sequence(
            signal.reshape(seq_count, length, own_width),
            expand_in,
            rate_in,
            damping_in,
            project_in,
            skip_in,
        )
        return mixed_rows.reshape(row_count, own_width)

    mixer_out, mixer_pull = jax.vjp(
        mixer_rows, normed_own, expand, ema_rate, damping, project, ema_skip
    )
    mixer_low = mixer_out.astype(jnp.bfloat16)
    shared_term = jnp.dot(mixer_low, w_shared, preferred_element_type=jnp.float32)
    reset_pre, update_pre, shared_pre = (
        lax.psum_scatter(
            jnp.dot(mixer_low, w_reset, preferred_element_type=jnp.float32),
            "tensor",
            scatter_dimension=1,
            tiled=True,
        ),
        lax.psum_scatter(
            jnp.dot(mixer_low, w_update, preferred_element_type=jnp.float32),
            "tensor",
            scatter_dimension=1,
            tiled=True,
        ),
        lax.psum_scatter(
            jnp.tile(shared_term, (1, tensor_count)), "tensor", scatter_dimension=1, tiled=True
        ),
    )
    shared = jax.nn.silu(shared_pre)
    queries = (shared * qk_affine[0] + qk_affine[1]).astype(jnp.bfloat16)
    keys_low = (shared * qk_affine[2]).astype(jnp.bfloat16)
    piece_ids = jax.vmap(partial(piece_ids_of, length=length))(piece_starts)
    query_seqs = queries.reshape(seq_count, length, shared_width)
    key_seqs = keys_low.reshape(seq_count, length, shared_width)
    value_seqs = values_low.reshape(seq_count, length, value_width)
    attended, log_total = lax.map(attend_forward, (query_seqs, key_seqs, value_seqs, piece_ids))
    attended = attended.reshape(row_count, value_width)
    reset_gate = jax.nn.silu(reset_pre)
    gated_low = (reset_gate * attended).astype(jnp.bfloat16)
    hidden_pre = lax.psum_scatter(
        jnp.dot(mixer_low, w_hidden, preferred_element_type=jnp.float32)
        + jnp.dot(gated_low, u_hidden, preferred_element_type=jnp.float32),
        "tensor",
        scatter_dimension=1,
        tiled=True,
    )
    candidate = jax.nn.silu(hidden_pre)
    update = jax.nn.sigmoid(update_pre)
    state_own = update * candidate + (1.0 - update) * inputs
    new_state, grad_full = (
        lax.all_gather(state_own, "tensor", axis=1, tiled=True),
        lax.all_gather(cotangent, "tensor", axis=1, tiled=True),
    )
    unit_state, inv_state = normalize_keep(new_state)
    state_low = (unit_state * norm_out).astype(jnp.bfloat16)
    ffn_pre = jnp.dot(state_low, w_in, preferred_element_type=jnp.float32)
    ffn_low = jax.nn.silu(ffn_pre).astype(jnp.bfloat16)
    branch = lax.psum_scatter(
        jnp.dot(ffn_low, w_out, preferred_element_type=jnp.float32).astype(jnp.bfloat16),
        "tensor",
        scatter_dimension=1,
        tiled=True,
    ).astype(jnp.float32)
    outputs = state_own + branch
    grad_low = grad_full.astype(jnp.bfloat16)
    grad_w_out = jnp.einsum("rf,rd->fd", ffn_low, grad_low, preferred_element_type=jnp.float32)
    grad_ffn = jnp.einsum("rd,fd->rf", grad_low, w_out, preferred_element_type=jnp.float32)
    grad_ffn_low = (grad_ffn * silu_grad(ffn_pre)).astype(jnp.bfloat16)
    grad_w_in = jnp.einsum("rd,rf->df", state_low, grad_ffn_low, preferred_element_type=jnp.float32)
    unit_term = jnp.einsum("rf,df->rd", grad_ffn_low, w_in, preferred_element_type=jnp.float32)
    unit_weighted = unit_term * norm_out
    unit_mean = jnp.mean(unit_weighted, axis=1, keepdims=True)
    unit_cross = jnp.mean(unit_weighted * unit_state, axis=1, keepdims=True)
    grad_unit, state_mean, state_cross = (
        lax.psum_scatter(
            unit_term.astype(jnp.bfloat16), "tensor", scatter_dimension=1, tiled=True
        ).astype(jnp.float32),
        lax.psum_scatter(
            jnp.tile(unit_mean, (1, tensor_count)).astype(jnp.bfloat16),
            "tensor",
            scatter_dimension=1,
            tiled=True,
        ).astype(jnp.float32),
        lax.psum_scatter(
            jnp.tile(unit_cross, (1, tensor_count)).astype(jnp.bfloat16),
            "tensor",
            scatter_dimension=1,
            tiled=True,
        ).astype(jnp.float32),
    )
    unit_own = lax.dynamic_slice_in_dim(unit_state, own_first, own_width, 1)
    norm_out_own = lax.dynamic_slice_in_dim(norm_out, own_first, own_width, 0)
    grad_norm_out = jnp.sum(grad_unit * unit_own, axis=0)
    grad_state = cotangent + inv_state * (
        grad_unit * norm_out_own - state_mean - unit_own * state_cross
    )
    update_grad_own = (grad_state * (candidate - inputs) * update * (1.0 - update)).astype(
        jnp.bfloat16
    )
    hidden_grad_own = (grad_state * update * silu_grad(hidden_pre)).astype(jnp.bfloat16)
    update_grad_low, hidden_grad_low = (
        lax.all_gather(update_grad_own, "tensor", axis=1, tiled=True),
        lax.all_gather(hidden_grad_own, "tensor", axis=1, tiled=True),
    )
    grad_w_update = jnp.einsum(
        "rc,rd->cd", mixer_low, update_grad_low, preferred_element_type=jnp.float32
    )
    grad_w_hidden = jnp.einsum(
        "rc,rd->cd", mixer_low, hidden_grad_low, preferred_element_type=jnp.float32
    )
    grad_u_hidden = jnp.einsum(
        "rv,rd->vd", gated_low, hidden_grad_low, preferred_element_type=jnp.float32
    )
    grad_gated = jnp.einsum(
        "rd,vd->rv", hidden_grad_low, u_hidden, preferred_element_type=jnp.float32
    )
    grad_attended = (grad_gated * reset_gate).astype(jnp.bfloat16)
    reset_grad_low = (grad_gated * attended * silu_grad(reset_pre)).astype(jnp.bfloat16)
    reset_grad_full = lax.all_gather(reset_grad_low, "tensor", axis=1, tiled=True)
    grad_w_reset = jnp.einsum(
        "rc,rv->cv", mixer_low, reset_grad_full, preferred_element_type=jnp.float32
    )
    query_grad, key_grad, value_grad = lax.map(
        attend_backward,
        (
            query_seqs,
            key_seqs,
            value_seqs,
            piece_ids,
            log_total,
            grad_attended.reshape(seq_count, length, value_width),
        ),
    )
    query_grad = query_grad.reshape(row_count, shared_width)
    key_grad = key_grad.reshape(row_count, shared_width)
    value_grad = value_grad.reshape(row_count, value_width)
    value_grad_low = (value_grad * silu_grad(value_pre)).astype(jnp.bfloat16)
    grad_w_value = jnp.einsum(
        "rd,rv->dv", normed_low, value_grad_low, preferred_element_type=jnp.float32
    )
    normed_term = jnp.einsum(
        "rv,dv->rd", value_grad_low, w_value, preferred_element_type=jnp.float32
    )
    shared_part = query_grad * qk_affine[0] + key_grad * qk_affine[2]
    affine_part = jnp.stack(
        [
            jnp.sum(query_grad * shared, axis=0),
            jnp.sum(query_grad, axis=0),
            jnp.sum(key_grad * shared, axis=0),
        ]
    )
    grad_shared, grad_qk_affine = (
        lax.psum(shared_part.astype(jnp.bfloat16), "tensor").astype(jnp.float32),
        lax.psum(affine_part.astype(jnp.bfloat16), "tensor").astype(jnp.float32),
    )
    shared_grad_low = (grad_shared * silu_grad(shared_pre)).astype(jnp.bfloat16)
    grad_w_shared = jnp.einsum(
        "rc,rz->cz", mixer_low, shared_grad_low, preferred_element_type=jnp.float32
    )
    grad_mixer = (
        jnp.einsum("rz,cz->rc", shared_grad_low, w_shared, preferred_element_type=jnp.float32)
        + jnp.einsum("rd,cd->rc", update_grad_low, w_update, preferred_element_type=jnp.float32)
        + jnp.einsum("rv,cv->rc", reset_grad_full, w_reset, preferred_element_type=jnp.float32)
        + jnp.einsum("rd,cd->rc", hidden_grad_low, w_hidden, preferred_element_type=jnp.float32)
    )
    ema_grad, grad_expand, grad_ema_rate, grad_damping, grad_project, grad_ema_skip = mixer_pull(
        grad_mixer
    )
    own_sum = lax.dynamic_slice_in_dim(normed_term, own_first, own_width, 1) + ema_grad
    normed_term = lax.dynamic_update_slice_in_dim(normed_term, own_sum, own_first, 1)
    normed_weighted = normed_term * norm_in
    normed_mean = jnp.mean(normed_weighted, axis=1, keepdims=True)
    normed_cross = jnp.mean(normed_weighted * unit_in, axis=1, keepdims=True)
    grad_normed, input_mean, input_cross = (
        lax.psum_scatter(
            normed_term.astype(jnp.bfloat16), "tensor", scatter_dimension=1, tiled=True
        ).astype(jnp.float32),
        lax.psum_scatter(
            jnp.tile(normed_mean, (1, tensor_count)).astype(jnp.bfloat16),
            "tensor",
            scatter_dimension=1,
            tiled=True,
        ).astype(jnp.float32),
        lax.psum_scatter(
            jnp.tile(normed_cross, (1, tensor_count)).astype(jnp.bfloat16),
            "tensor",
            scatter_dimension=1,
            tiled=True,
        ).astype(jnp.float32),
    )
    unit_in_own = lax.dynamic_slice_in_dim(unit_in, own_first, own_width, 1)
    norm_in_own = lax.dynamic_slice_in_dim(norm_in, own_first, own_width, 0)
    grad_norm_in = jnp.sum(grad_normed * unit_in_own, axis=0)
    grad_inputs = grad_state * (1.0 - update) + inv_in * (
        grad_normed * norm_in_own - input_mean - unit_in_own * input_cross
    )
    small_summed = lax.psum(
        (
            grad_norm_in,
            grad_expand,
            grad_ema_rate,
            grad_damping,
            grad_project,
            grad_ema_skip,
            grad_norm_out,
            grad_qk_affine,
        ),
        "dp",
    )
    matrix_summed = (
        lax.psum_scatter(grad_w_value, "dp", scatter_dimension=0, tiled=True),
        lax.psum_scatter(grad_w_shared, "dp", scatter_dimension=1, tiled=True),
        lax.psum_scatter(grad_w_reset, "dp", scatter_dimension=1, tiled=True),
        lax.psum_scatter(grad_w_update, "dp", scatter_dimension=1, tiled=True),
        lax.psum_scatter(grad_w_hidden, "dp", scatter_dimension=1, tiled=True),
        lax.psum_scatter(grad_u_hidden, "dp", scatter_dimension=1, tiled=True),
        lax.psum_scatter(grad_w_in, "dp", scatter_dimension=0, tiled=True),
        lax.psum_scatter(grad_w_out, "dp", scatter_dimension=1, tiled=True),
    )
    return (
        outputs,
        grad_inputs,
        small_summed[0],
        matrix_summed[0],
        small_summed[1],
        small_summed[2],
        small_summed[3],
        small_summed[4],
        small_summed[5],
        matrix_summed[1],
        small_summed[7],
        matrix_summed[2],
        matrix_summed[3],
        matrix_summed[4],
        matrix_summed[5],
        small_summed[6],
        matrix_summed[6],
        matrix_summed[7],
    )


def solution(mesh):
    placed = (
        P("dp", "tensor"),
        P(),
        P(None, "tensor"),
        P("tensor", None),
        P("tensor", None),
        P("tensor", None),
        P("tensor", None),
        P("tensor"),
        P("tensor", None),
        P(),
        P("tensor", None),
        P("tensor", None),
        P("tensor", None),
        P("tensor", None),
        P(),
        P(None, "tensor"),
        P("tensor", None),
        P("dp", "tensor"),
        P("dp", None),
    )
    return jax.shard_map(
        on_device,
        mesh=mesh,
        in_specs=placed,
        out_specs=(
            P("dp", "tensor"),
            P("dp", "tensor"),
            P("tensor"),
            P("dp", "tensor"),
            P("tensor", None),
            P("tensor", None),
            P("tensor", None),
            P("tensor", None),
            P("tensor"),
            P("tensor", "dp"),
            P(),
            P("tensor", "dp"),
            P("tensor", "dp"),
            P("tensor", "dp"),
            P("tensor", "dp"),
            P("tensor"),
            P("dp", "tensor"),
            P("tensor", "dp"),
        ),
        check_vma=False,
    )
```

profile of v0, /device:TPU:10, one launch (start us, length us, event | category | flops | bytes accessed | tf_op | source)
XLA Modules:
  0.0 1380.1 jit_solution(12030416727049386802)
XLA Ops:
  17.6 16.1 %gather_fusion = f32[4096,256]{1,0:T(8,128)} fusion(f32[64,256]{1,0:T(8,128)S(1)} %copy.166, s32[4096]{0:T(1024)S(1)} %broadcast_clamp_fusion), kind=kCustom, calls=%fused_computation | custom fusion | bytes 8404992 | tf_op jit(solution)/shard_map/jvp(vmap(jit(_take)))/gather | solution.py:21
  33.7 9.2 copy.167
  43.0 46.1 %all-gather.7.cloned.1.call-done = f32[1024,1024]{1,0:T(8,128)} async-done(((f32[1024,256]{1,0:T(8,128)}), f32[1024,1024]{1,0:T(8,128)}) %all-gather.7.cloned.1.call-update) | async-done | bytes 4194320 | tf_op jit(solution)/shard_map/all_gather | solution.py:180
  115.2 16.0 %fusion.21 = f32[256,16,64]{2,1,0:T(8,128)S(1)} fusion(f32[16,64,256]{1,0,2:T(8,128)} %copy.168, f32[64,64,256]{1,0,2:T(8,128)} %copy.167, pred[64,64]{1,0:T(8,128)(4,1)S(1)} %get-tuple-element.666, pred[64,64]{1,0:T(8,128)(4,1)S(1)} %get-tuple-element.667), kind=kOutput, calls=%fused_computation.48 | convolution fusion | flops 203423744 | bytes 6299648 | tf_op jit(solution)/shard_map/jvp(vmap(ijc,njc->nic))/dot_general | solution.py:37
  163.9 24.5 %reduce-scatter.20.cloned.1.call-done = f32[1024,128]{1,0:T(8,128)} async-done(((f32[1024,512]{1,0:T(8,128)}), f32[1024,128]{1,0:T(8,128)}) %reduce-scatter.20.cloned.1.call-update) | async-done | bytes 524304 | tf_op jit(solution)/shard_map/reduce_scatter | solution.py:218
  190.4 14.6 %while.79 = (s32[]{:T(128)}, f32[2,512,512]{2,1,0:T(8,128)}, f32[2,512]{1,0:T(2,128)S(1)}, s32[2]{0:T(128)S(1)}, s32[1024]{0:T(1024)S(1)}, /*index=5*/bf16[1024,...) while((s32[]{:T(128)}, f32[2,512,512]{2,1,0:T(8,128)}, ...), condition=%wide.region_12.13_spmd, body=%wide.region_9.12_spmd.sunk | while | flops 677380608 | bytes 25595140 | solution.py:105
  205.1 131.6 %reduce-scatter.18.cloned.1.call-done = f32[1024,512]{1,0:T(8,128)} async-done(((f32[1024,2048]{1,0:T(8,128)}), f32[1024,512]{1,0:T(8,128)}) %reduce-scatter.18.cloned.1.call-update) | async-done | bytes 2097168 | tf_op jit(solution)/shard_map/reduce_scatter | solution.py:206
  344.1 72.6 %reduce-scatter.16.cloned.1.call-done = f32[1024,256]{1,0:T(8,128)} async-done(((f32[1024,1024]{1,0:T(8,128)}), f32[1024,256]{1,0:T(8,128)}) %reduce-scatter.16.cloned.1.call-update) | async-done | bytes 1048592 | tf_op jit(solution)/shard_map/reduce_scatter | solution.py:212
  416.7 79.4 %reduce-scatter.22.cloned.1.call-done = f32[1024,256]{1,0:T(8,128)} async-done(((f32[1024,1024]{1,0:T(8,128)}), f32[1024,256]{1,0:T(8,128)}) %reduce-scatter.22.cloned.1.call-update) | async-done | bytes 1048592 | tf_op jit(solution)/shard_map/reduce_scatter | solution.py:233
  501.6 76.6 %all-gather.9.cloned.1.call-done = f32[1024,1024]{1,0:T(8,128)} async-done(((f32[1024,256]{1,0:T(8,128)}), f32[1024,1024]{1,0:T(8,128)}) %all-gather.9.cloned.1.call-update) | async-done | bytes 4194320 | tf_op jit(solution)/shard_map/all_gather | solution.py:244
  590.9 34.1 %all-gather.11.cloned.1.call-done = bf16[1024,1024]{1,0:T(8,128)(2,1)} async-done(((bf16[1024,256]{1,0:T(8,128)(2,1)}), bf16[1024,1024]{1,0:T(8,128)(2,1)}) %all-gather.11.cloned.1.call-update) | async-done | bytes 2097168 | tf_op jit(solution)/shard_map/all_gather | solution.py:245
  637.1 17.1 %all-reduce.6 = (bf16[1024,4]{0,1:T(4,128)(2,1)S(1)}, bf16[1024,4]{0,1:T(4,128)(2,1)S(1)}) all-reduce(bf16[1024,4]{0,1:T(4,128)(2,1)S(1)} %tile.15, bf16[1024,4]{0,1:T(4,128)(2,1)S(1)} %tile.14), channel_id=9, replica_groups=mesh['dp'=8,'tensor'=4] {'tensor'}, use_global_device_ids=true, to_apply=%region_21.22.clone | all-reduce | flops 8192 | bytes 32768
  655.5 24.5 %reduce-scatter.26.cloned.1.call-done = bf16[1024,256]{1,0:T(8,128)(2,1)} async-done(((bf16[1024,1024]{1,0:T(8,128)(2,1)}), bf16[1024,256]{1,0:T(8,128)(2,1)}) %reduce-scatter.26.cloned.1.call-update) | async-done | bytes 524304 | tf_op jit(solution)/shard_map/reduce_scatter | solution.py:268
  686.1 43.2 %all-gather.13.cloned.1.call-done = bf16[1024,1024]{1,0:T(8,128)(2,1)} async-done(((bf16[1024,256]{1,0:T(8,128)(2,1)}), bf16[1024,1024]{1,0:T(8,128)(2,1)}) %all-gather.13.cloned.1.call-update) | async-done | bytes 2097168 | tf_op jit(solution)/shard_map/all_gather | solution.py:296
  735.5 22.2 %while.81 = (s32[]{:T(128)}, f32[1024,128]{1,0:T(8,128)}, f32[1024,512]{1,0:T(8,128)}, f32[2,512,128]{2,1,0:T(8,128)}, s32[2]{0:T(128)S(1)}, /*index=5*/s32[1024...) while((s32[]{:T(128)}, f32[1024,128]{1,0:T(8,128)}, ...), condition=%wide.region_24.25_spmd.clone, body=%wide.region_22.24_spmd.clone.sunk | while | flops 2828272128 | bytes 53767648 | solution.py:144
  779.9 34.5 %all-reduce.10.cloned.1.call-done = bf16[1024,128]{1,0:T(8,128)(2,1)} async-done(((bf16[1024,128]{1,0:T(8,128)(2,1)}), bf16[1024,128]{1,0:T(8,128)(2,1)}) %all-reduce.10.cloned.1.call-update) | async-done | bytes 262160 | tf_op jit(solution)/shard_map/psum | solution.py:346
  815.6 78.5 %all-gather.17.cloned.1.call-done = bf16[1024,2048]{1,0:T(8,128)(2,1)} async-done(((bf16[1024,512]{1,0:T(8,128)(2,1)}), bf16[1024,2048]{1,0:T(8,128)(2,1)}) %all-gather.17.cloned.1.call-update) | async-done | bytes 4194320 | tf_op jit(solution)/shard_map/all_gather | solution.py:312
  910.5 23.4 %while.82 = (s32[]{:T(128)}, f32[256,16]{0,1:T(8,128)S(1)}, f32[1,256,16]{1,2,0:T(8,128)S(1)}, f32[16,1,256,16]{2,3,1,0:T(8,128)S(1)}, f32[16,1,256,16]{2,3,1,0:...) while((s32[]{:T(128)}, f32[256,16]{0,1:T(8,128)S(1)}, ...), condition=%wide.region_27.28_spmd.clone, body=%wide.region_26.27_spmd.clone.sunk | while | flops 32772 | bytes 165516 | solution.py:46
  936.4 10.6 fusion.20
  965.2 7.4 fusion.82
  973.3 7.2 fusion.98
  1020.7 17.6 %all-reduce.5 = (bf16[3,128]{1,0:T(4,128)(2,1)}, bf16[1024,4]{0,1:T(4,128)(2,1)}, bf16[1024,4]{0,1:T(4,128)(2,1)}) all-reduce(bf16[3,128]{1,0:T(4,128)(2,1)S(1)} %pad_maximum_fusion, bf16[1024,4]{0,1:T(4,128)(2,1)S(1)} %tile.17, bf16[1024,4]{0,1:T(4,128)(2,1)S(1)} %tile.16), channel_id=1, replica_groups=mesh['dp'=8,'tensor'=4] {'tensor'}, use_global_device_ids=true, to_apply=%region_51.52 | all-reduce | flops 8576 | bytes 34304 | tf_op jit(solution)/shard_map/psum | solution.py:347
  1038.4 16.6 %select_bitcast_fusion = f32[64,64,256]{1,0,2:T(8,128)} fusion(pred[64,64]{1,0:T(8,128)(4,1)S(1)} %copy-done.63, f32[16,64,256]{1,0,2:T(8,128)S(1)} %copy-done.5, f32[1,16,64,256]{2,1,3,0:T(8,128)} %copy-done.14), kind=kOutput, calls=%fused_computation.45 | convolution fusion | flops 202375168 | bytes 6295552 | tf_op jit(solution)/shard_map/transpose(jvp(vmap(ijc,njc->nic)))/dot_general | solution.py:37
  1055.0 8.2 copy.187
  1063.2 25.2 %scatter_custom_fusion = f32[64,256]{1,0:T(8,128)S(1)} fusion(s32[4096]{0:T(1024)} %copy-done.67, f32[4096,256]{1,0:T(8,128)} %bitcast.240, f32[]{:T(128)} %constant.192.clone.1), kind=kCustom, calls=%fused_computation.175 | custom fusion | flops 1048576 | bytes 66048 | tf_op jit(solution)/shard_map/transpose(jvp(vmap(jit(_take))))/scatter-add | solution.py:21
  1106.8 22.4 %all-reduce.11 = (f32[256]{0:T(256)}, f32[256,16]{0,1:T(8,128)}, f32[256,16]{0,1:T(8,128)}, f32[256,16]{0,1:T(8,128)}, f32[256,16]{0,1:T(8,128)}, /*index=5*/f32[256]{0:T(256)}, f32[3,128]{1,0:T(4,128)}, f32[256]{0:T(256)}) all-reduce(f32[256]{0:T(256)S(1)} %get-tuple-element.639, ...), channel_id=1, replica_groups=mesh['dp'=8,'tensor'=4] {'dp'}, use_global_device_ids=true, to_apply=%region_34.35 | all-reduce | flops 17536 | bytes 139520 | tf_op jit(solution)/shard_map/psum | solution.py:390
  1129.2 28.7 %reduce-scatter.32.cloned.1.call-done = f32[256,16]{0,1:T(8,128)} async-done(((f32[256,128]{0,1:T(8,128)}), f32[256,16]{0,1:T(8,128)}) %reduce-scatter.32.cloned.1.call-update) | async-done | bytes 16400 | tf_op jit(solution)/shard_map/reduce_scatter | solution.py:405
  1157.8 39.6 %reduce-scatter.38.cloned.1.call-done = f32[256,128]{1,0:T(8,128)} async-done(((f32[256,1024]{1,0:T(8,128)}), f32[256,128]{1,0:T(8,128)}) %reduce-scatter.38.cloned.1.call-update) | async-done | bytes 131088 | tf_op jit(solution)/shard_map/reduce_scatter | solution.py:408
  1197.5 39.8 %reduce-scatter.36.cloned.1.call-done = f32[256,128]{1,0:T(8,128)} async-done(((f32[256,1024]{1,0:T(8,128)}), f32[256,128]{1,0:T(8,128)}) %reduce-scatter.36.cloned.1.call-update) | async-done | bytes 131088 | tf_op jit(solution)/shard_map/reduce_scatter | solution.py:407
  1237.2 44.9 %reduce-scatter.40.cloned.1.call-done = f32[512,128]{1,0:T(8,128)} async-done(((f32[512,1024]{1,0:T(8,128)}), f32[512,128]{1,0:T(8,128)}) %reduce-scatter.40.cloned.1.call-update) | async-done | bytes 262160 | tf_op jit(solution)/shard_map/reduce_scatter | solution.py:409
  1282.2 45.5 %reduce-scatter.30.cloned.1.call-done = f32[128,512]{1,0:T(8,128)} async-done(((f32[1024,512]{1,0:T(8,128)}), f32[128,512]{1,0:T(8,128)}) %reduce-scatter.30.cloned.1.call-update) | async-done | bytes 262160 | tf_op jit(solution)/shard_map/reduce_scatter | solution.py:404
  1327.6 45.1 %reduce-scatter.34.cloned.1.call-done = f32[256,256]{1,0:T(8,128)} async-done(((f32[256,2048]{1,0:T(8,128)}), f32[256,256]{1,0:T(8,128)}) %reduce-scatter.34.cloned.1.call-update) | async-done | bytes 262160 | tf_op jit(solution)/shard_map/reduce_scatter | solution.py:406
  (483 shorter events, 298.7 us)
Async XLA Ops:
  7.2 579.5 %copy-start = (bf16[1024,1024]{1,0:T(8,128)(2,1)S(1)}, bf16[1024,1024]{1,0:T(8,128)(2,1)}, u32[]{:S(2)}) copy-start(bf16[1024,1024]{1,0:T(8,128)(2,1)} %param.42) | copy-start | bytes 6291460
  7.2 81.9 %all-gather.7.cloned.1.call-start = ((), (), s32[]{:S(2)}) async-start(), calls=%async_computation.15 | async-start | bytes 5242880 | tf_op jit(solution)/shard_map/all_gather | solution.py:180
  7.9 180.4 %reduce-scatter.20.cloned.1.call-start = ((), (), s32[]{:S(2)}) async-start(), calls=%async_computation.18 | async-start | bytes 2621440 | tf_op jit(solution)/shard_map/reduce_scatter | solution.py:218
  9.6 121.7 %copy-start.41 = (f32[256,16]{1,0:T(8,128)}, f32[256,16]{1,0:T(8,128)S(1)}, u32[]{:S(2)}) copy-start(f32[256,16]{1,0:T(8,128)S(1)} %copy.164) | copy-start | bytes 49156
  10.5 91.8 %copy-start.35 = (f32[256,16]{1,0:T(8,128)}, f32[256,16]{1,0:T(8,128)S(1)}, u32[]{:S(2)}) copy-start(f32[256,16]{1,0:T(8,128)S(1)} %copy.169) | copy-start | bytes 49156
  10.6 120.7 %copy-start.73 = (f32[64]{0:T(128)}, f32[64]{0:T(128)S(1)}, u32[]{:S(2)}) copy-start(f32[64]{0:T(128)S(1)} %iota_convert_fusion) | copy-start | bytes 772
  145.6 191.0 %reduce-scatter.18.cloned.1.call-start = ((), (), s32[]{:S(2)}) async-start(), calls=%async_computation.17 | async-start | bytes 10485760 | tf_op jit(solution)/shard_map/reduce_scatter | solution.py:206
  151.9 264.8 %reduce-scatter.16.cloned.1.call-start = ((), (), s32[]{:S(2)}) async-start(), calls=%async_computation.16 | async-start | bytes 5242880 | tf_op jit(solution)/shard_map/reduce_scatter | solution.py:212
  155.7 340.4 %reduce-scatter.22.cloned.1.call-start = ((), (), s32[]{:S(2)}) async-start(), calls=%async_computation.19 | async-start | bytes 5242880 | tf_op jit(solution)/shard_map/reduce_scatter | solution.py:233
  205.1 134.6 %copy-start.58 = (bf16[1024,128]{1,0:T(8,128)(2,1)}, bf16[1024,128]{1,0:T(8,128)(2,1)S(1)}, u32[]{:S(2)}) copy-start(bf16[1024,128]{1,0:T(8,128)(2,1)S(1)} %get-tuple-element.1096) | copy-start | bytes 786436
  344.0 152.1 %copy-start.27 = (f32[1024,256]{1,0:T(8,128)S(1)}, f32[1024,256]{1,0:T(8,128)}, u32[]{:S(2)}) copy-start(f32[1024,256]{1,0:T(8,128)} %param.27) | copy-start | bytes 3145732
  344.0 234.2 %all-gather.9.cloned.1.call-start = ((), (), s32[]{:S(2)}) async-start(), calls=%async_computation.20 | async-start | bytes 5242880 | tf_op jit(solution)/shard_map/all_gather | solution.py:244
  499.3 125.8 %all-gather.11.cloned.1.call-start = ((), (), s32[]{:S(2)}) async-start(), calls=%async_computation.22 | async-start | bytes 2621440 | tf_op jit(solution)/shard_map/all_gather | solution.py:245
  501.4 178.6 %reduce-scatter.26.cloned.1.call-start = ((), (), s32[]{:S(2)}) async-start(), calls=%async_computation.23 | async-start | bytes 2621440 | tf_op jit(solution)/shard_map/reduce_scatter | solution.py:268
  635.8 93.6 %all-gather.13.cloned.1.call-start = ((), (), s32[]{:S(2)}) async-start(), calls=%async_computation.24 | async-start | bytes 2621440 | tf_op jit(solution)/shard_map/all_gather | solution.py:296
  685.3 91.1 %all-gather.15.cloned.1.call-start = ((), (), s32[]{:S(2)}) async-start(), calls=%async_computation.26 | async-start | bytes 2621440 | tf_op jit(solution)/shard_map/all_gather | solution.py:295
  685.8 128.5 %all-reduce.10.cloned.1.call-start = ((), (), s32[]{:S(2)}) async-start(), calls=%async_computation.25 | async-start | bytes 524288 | tf_op jit(solution)/shard_map/psum | solution.py:346
  760.7 133.4 %all-gather.17.cloned.1.call-start = ((), (), s32[]{:S(2)}) async-start(), calls=%async_computation.27 | async-start | bytes 5242880 | tf_op jit(solution)/shard_map/all_gather | solution.py:312
  761.2 243.3 %reduce-scatter.24.cloned.1.call-start = ((), (), s32[]{:S(2)}) async-start(), calls=%async_computation.21 | async-start | bytes 2621440 | tf_op jit(solution)/shard_map/reduce_scatter | solution.py:251
  767.3 336.0 %reduce-scatter.28.cloned.1.call-start = ((), (), s32[]{:S(2)}) async-start(), calls=%async_computation.28 | async-start | bytes 2621440 | tf_op jit(solution)/shard_map/reduce_scatter | solution.py:368
  776.4 117.7 %copy-start.49 = (bf16[256,2048]{1,0:T(8,128)(2,1)S(1)}, bf16[256,2048]{1,0:T(8,128)(2,1)}, u32[]{:S(2)}) copy-start(bf16[256,2048]{1,0:T(8,128)(2,1)} %param.37) | copy-start | bytes 3145732
  815.6 82.1 %copy-start.51 = (bf16[1024,128]{1,0:T(8,128)(2,1)}, bf16[1024,128]{1,0:T(8,128)(2,1)S(1)}, u32[]{:S(2)}) copy-start(bf16[1024,128]{1,0:T(8,128)(2,1)S(1)} %multiply_convert_fusion.11) | copy-start | bytes 786436
  815.6 82.1 %copy-start.66 = (bf16[256,128]{1,0:T(8,128)(2,1)S(1)}, bf16[256,128]{1,0:T(8,128)(2,1)}, u32[]{:S(2)}) copy-start(bf16[256,128]{1,0:T(8,128)(2,1)} %param.35) | copy-start | bytes 196612
  965.2 164.0 %reduce-scatter.44.cloned.1.call-start = ((), (), s32[]{:S(2)}) async-start(), calls=%async_computation.36 | async-start | bytes 4718592 | tf_op jit(solution)/shard_map/reduce_scatter | solution.py:411
  972.6 156.5 %reduce-scatter.42.cloned.1.call-start = ((), (), s32[]{:S(2)}) async-start(), calls=%async_computation.35 | async-start | bytes 4718592 | tf_op jit(solution)/shard_map/reduce_scatter | solution.py:410
  980.5 177.3 %reduce-scatter.32.cloned.1.call-start = ((), (), s32[]{:S(2)}) async-start(), calls=%async_computation.30 | async-start | bytes 147456 | tf_op jit(solution)/shard_map/reduce_scatter | solution.py:405
  982.6 214.9 %reduce-scatter.38.cloned.1.call-start = ((), (), s32[]{:S(2)}) async-start(), calls=%async_computation.33 | async-start | bytes 1179648 | tf_op jit(solution)/shard_map/reduce_scatter | solution.py:408
  986.2 251.1 %reduce-scatter.36.cloned.1.call-start = ((), (), s32[]{:S(2)}) async-start(), calls=%async_computation.32 | async-start | bytes 1179648 | tf_op jit(solution)/shard_map/reduce_scatter | solution.py:407
  989.7 292.5 %reduce-scatter.40.cloned.1.call-start = ((), (), s32[]{:S(2)}) async-start(), calls=%async_computation.34 | async-start | bytes 2359296 | tf_op jit(solution)/shard_map/reduce_scatter | solution.py:409
  994.0 333.7 %reduce-scatter.30.cloned.1.call-start = ((), (), s32[]{:S(2)}) async-start(), calls=%async_computation.29 | async-start | bytes 2359296 | tf_op jit(solution)/shard_map/reduce_scatter | solution.py:404
  998.9 373.8 %reduce-scatter.34.cloned.1.call-start = ((), (), s32[]{:S(2)}) async-start(), calls=%async_computation.31 | async-start | bytes 2359296 | tf_op jit(solution)/shard_map/reduce_scatter | solution.py:406
  1103.3 269.4 %copy-start.1 = (bf16[1024,1024]{1,0:T(8,128)(2,1)S(1)}, bf16[1024,1024]{1,0:T(8,128)(2,1)}, u32[]{:S(2)}) copy-start(bf16[1024,1024]{1,0:T(8,128)(2,1)} %param.42) | copy-start | bytes 6291460
  (90 other events, 682.0 us)
Sparse Core Ops, SparseCore 0:
  9.6 79.4 all-gather.6
  145.8 42.5 reduce-scatter.19
  190.8 145.7 reduce-scatter.17
  338.9 77.7 reduce-scatter.15
  418.8 77.2 reduce-scatter.21
  499.4 78.8 all-gather.8
  580.5 44.4 all-gather.10
  635.9 44.0 reduce-scatter.25
  685.4 43.9 all-gather.12
  730.7 44.4 all-gather.14
  778.2 36.1 all-reduce.9
  815.9 78.0 all-gather.16
  896.4 42.5 reduce-scatter.23
  965.3 42.5 reduce-scatter.27
  1012.0 52.8 reduce-scatter.43
  1068.7 51.5 reduce-scatter.41
  1124.1 33.7 reduce-scatter.31
  1161.4 35.9 reduce-scatter.37
  1201.2 35.9 reduce-scatter.35
  1240.9 41.1 reduce-scatter.39
  1286.4 41.2 reduce-scatter.29
  1331.5 41.2 reduce-scatter.33
where the time goes:
time: 1390 us; the launch traced here: 1380 us
  waiting for transfers between devices  891 us (64%)
  matrix products  197 us (14%)
  other arithmetic  115 us (8%)
  local copies, waits for them, and re-layouts  98.1 us (7%)
  blocking collectives  57.1 us (4%)
  between operations  15.8 us (1%)
    reduce_scatter x1, waiting for transfers between devices, on_device(): lax.psum_scatter(jnp.dot(mixer_low, w_reset, preferred_element_type=jnp.f...  132 us
    reduce_scatter x1, waiting for transfers between devices, on_device(): lax.psum_scatter(jnp.dot(mixer_low, w_hidden, preferred_element_type=jnp....  79.4 us
    all_gather x1, waiting for transfers between devices, on_device(): lax.all_gather(reset_grad_low, 'tensor', axis=1, tiled=True)  78.5 us
    all_gather x1, waiting for transfers between devices, on_device(): lax.all_gather(state_own, 'tensor', axis=1, tiled=True)  76.6 us
    reduce_scatter x1, waiting for transfers between devices, on_device(): lax.psum_scatter(jnp.dot(mixer_low, w_update, preferred_element_type=jnp....  72.6 us
    all_gather x1, waiting for transfers between devices, on_device(): full_in = lax.all_gather(inputs, 'tensor', axis=1, tiled=True)  46.1 us
    reduce_scatter x1, waiting for transfers between devices, on_device(): lax.psum_scatter(grad_w_value, 'dp', scatter_dimension=0, tiled=True)  45.5 us
    reduce_scatter x1, waiting for transfers between devices, on_device(): lax.psum_scatter(grad_w_reset, 'dp', scatter_dimension=1, tiled=True)  45.1 us
  transfers between devices with their start and end apart: 22, of which 17 were waited for; matrix products, arithmetic and copies ran while one was open for 23% of the time, Pallas kernels for 0%

commit v1 on v0

v1 whole, which is shorter than its diff:
```python
import jax
import jax.numpy as jnp
import numpy as np
from jax import lax
from jax.experimental import pallas as pl
from jax.experimental.pallas import tpu as pltpu
from jax.sharding import Mesh, PartitionSpec as P

f32 = jnp.float32
bf16 = jnp.bfloat16
PIECE = 256
EPS = 1e-5
HD = 16
CH = 8
LT = 128

GROUP = ("xx", "core", "tensor")
PLANE = ("yy", "xx")
DPS = ("yy", "xx", "rest", "core")
ALL = DPS + ("tensor",)

VM = pl.BlockSpec(memory_space=pltpu.VMEM)
SM = pl.BlockSpec(memory_space=pltpu.SMEM)


def shape(dims, dtype):
    return jax.ShapeDtypeStruct(tuple(dims), dtype)


def call(body, outs, idx, *args, name, scratch=(), flops=0, limit=48):
    return pl.pallas_call(
        body,
        out_shape=tuple(outs),
        in_specs=[SM] + [VM] * len(args),
        out_specs=(VM,) * len(outs),
        scratch_shapes=list(scratch),
        name=name,
        compiler_params=pltpu.CompilerParams(vmem_limit_bytes=limit << 20),
    )(idx, *args)


def dot(a, b):
    return jnp.dot(a, b, preferred_element_type=f32)


def dot_t(a, b):
    return lax.dot_general(a, b, (((1,), (1,)), ((), ())), preferred_element_type=f32)


def t_dot(a, b):
    return lax.dot_general(a, b, (((0,), (0,)), ((), ())), preferred_element_type=f32)


def sig(v):
    return 1.0 / (1.0 + jnp.exp(-v))


def silu(v):
    return v * sig(v)


def silu_grad(v):
    s = sig(v)
    return s * (1.0 + v * (1.0 - s))


def at(i, n):
    return pl.ds(pl.multiple_of(i * n, n), n)


def _params(par_ref, lanes):
    expand = par_ref[0:16, lanes]; rate = par_ref[16:32, lanes]
    damp = par_ref[32:48, lanes]; proj = par_ref[48:64, lanes]
    dec = 1.0 - rate*damp
    coef = proj*rate*expand
    return expand, rate, damp, proj, dec, coef

def _rows(a):
    return [jnp.broadcast_to(a[h:h+1], (CH, LT)) for h in range(HD)]

def _pow(a, n):
    out=None; base=a
    while n:
        if n&1: out = base if out is None else out*base
        n >>= 1
        if n: base = base*base
    return out

def _carry_down(s, decl):
    row = lax.broadcasted_iota(jnp.int32, (CH, LT), 0)
    out=[]
    for h in range(HD):
        v = s[h]; p = decl[h]
        for d in (1,2,4):
            v = v + p*jnp.where(row >= d, pltpu.roll(v, d, 0), 0.0)
            p = p*p
        out.append(jnp.where(row >= 1, pltpu.roll(v, 1, 0), 0.0))
    return out

def _carry_up(s, decl):
    row = lax.broadcasted_iota(jnp.int32, (CH, LT), 0)
    out=[]
    for h in range(HD):
        v = s[h]; p = decl[h]
        for d in (1,2,4):
            v = v + p*jnp.where(row < CH-d, pltpu.roll(v, CH-d, 0), 0.0)
            p = p*p
        out.append(jnp.where(row < CH-1, pltpu.roll(v, CH-1, 0), 0.0))
    return out

def fwd_kernel(x_ref, par_ref, skip_ref, m_ref, low_ref, s0_ref, xs, ms):
    T, W = x_ref.shape
    L = T//CH
    for lt in range(W//LT):
        lanes = slice(lt*LT, (lt+1)*LT)
        *_, dec, coef = _params(par_ref, lanes)
        dec = _rows(dec); coef=_rows(coef)
        skip = jnp.broadcast_to(skip_ref[0:1, lanes], (CH, LT))
        z = jnp.zeros((CH,LT), f32)
        xs[...] = x_ref[:, lanes]
        def one(i, s):
            xi = xs[pl.ds(i, CH, stride=L), :]
            return tuple(dec[h]*s[h]+xi for h in range(HD))
        s = lax.fori_loop(0, L, one, (z,)*HD, unroll=8)
        s0 = _carry_down(s, [_pow(dec[h], L) for h in range(HD)])
        for h in range(HD):
            s0_ref[h, :, lanes] = s0[h]
        def two(i, s):
            xi = xs[pl.ds(i, CH, stride=L), :]
            s = tuple(dec[h]*s[h]+xi for h in range(HD))
            y = skip*xi
            terms=[coef[h]*s[h] for h in range(HD)]
            while len(terms)>1:
                terms=[terms[k]+terms[k+1] for k in range(0,len(terms),2)]
            ms[pl.ds(i, CH, stride=L), :] = y+terms[0]
            return s
        lax.fori_loop(0, L, two, tuple(s0), unroll=4)
        m_ref[:, lanes] = ms[...]
        low_ref[:, lanes] = silu(ms[...]).astype(bf16)

def bwd_kernel(g_ref, m_ref, x_ref, par_ref, skip_ref, s0_ref, eg_ref, gp_ref, gm_ref, st_ref, xs, gs_ref, es):
    T, W = x_ref.shape
    L = T//CH
    for lt in range(W//LT):
        lanes = slice(lt*LT, (lt+1)*LT)
        expand, rate, damp, proj, dec2, coef2 = _params(par_ref, lanes)
        dec=_rows(dec2); coef=_rows(coef2)
        skip = jnp.broadcast_to(skip_ref[0:1, lanes], (CH, LT))
        z = jnp.zeros((CH,LT), f32)
        xs[...] = x_ref[:, lanes]
        m = m_ref[:, lanes]
        sg = 1.0/(1.0+jnp.exp(-m))
        gs_ref[...] = g_ref[:, lanes].astype(f32)*(sg*(1.0+m*(1.0-sg)))
        def one(k, c):
            b, gs = c
            i = L-1-k
            gm = gs_ref[pl.ds(i, CH, stride=L), :]
            gm_ref[i] = gm
            xi = xs[pl.ds(i, CH, stride=L), :]
            gs = gs + gm*xi
            return (tuple(dec[h]*b[h]+gm for h in range(HD)), gs)
        b, gs = lax.fori_loop(0, L, one, ((z,)*HD, z), unroll=4)
        e = _carry_up(b, [_pow(dec[h], L) for h in range(HD)])
        s0 = [s0_ref[h, :, lanes] for h in range(HD)]
        for h in range(HD): st_ref[0, h] = s0[h]
        def rec(i, s):
            xi = xs[pl.ds(i, CH, stride=L), :]
            s = tuple(dec[h]*s[h]+xi for h in range(HD))
            for h in range(HD): st_ref[i+1, h] = s[h]
            return s
        lax.fori_loop(0, L, rec, tuple(s0), unroll=4)
        gcoef=[]; gdec=[]
        G=8
        for g0 in range(0, HD, G):
            hs = range(g0, g0+G)
            def two(k, c):
                b, gc, gd = c
                i = L-1-k
                gm = gm_ref[i]
                b = tuple(dec[h]*b[j]+gm for j,h in enumerate(hs))
                gc = tuple(gc[j]+gm*st_ref[i+1,h] for j,h in enumerate(hs))
                gd = tuple(gd[j]+b[j]*st_ref[i,h] for j,h in enumerate(hs))
                terms=[coef[h]*b[j] for j,h in enumerate(hs)]
                while len(terms)>1:
                    terms=[terms[q]+terms[q+1] for q in range(0,len(terms),2)]
                if g0==0: base = skip*gm
                else: base = es[pl.ds(i, CH, stride=L), :]
                es[pl.ds(i, CH, stride=L), :] = base+terms[0]
                return (b, gc, gd)
            zz=(z,)*G
            _, gc, gd = lax.fori_loop(0, L, two, (tuple(e[h] for h in hs), zz, zz), unroll=2)
            gcoef += list(gc); gdec += list(gd)
        eg_ref[:, lanes] = es[...]
        gcoef = jnp.concatenate([jnp.sum(v,0,keepdims=True) for v in gcoef],0)
        gdec = jnp.concatenate([jnp.sum(v,0,keepdims=True) for v in gdec],0)*coef2
        gp_ref[0:16, lanes] = gcoef*proj*rate
        gp_ref[16:32, lanes] = gcoef*proj*expand - gdec*damp
        gp_ref[32:48, lanes] = -gdec*rate
        gp_ref[48:64, lanes] = gcoef*rate*expand
        gp_ref[64:72, lanes] = jnp.broadcast_to(jnp.sum(gs,0,keepdims=True),(8,LT))

def ema_fwd(x, par, skip):
    T,W = x.shape
    return pl.pallas_call(fwd_kernel, out_shape=(jax.ShapeDtypeStruct((T,W),f32), jax.ShapeDtypeStruct((T,W),bf16), jax.ShapeDtypeStruct((HD,CH,W),f32)),
        in_specs=[VM]*3, out_specs=(VM,VM,VM), name="ema_fwd", scratch_shapes=[pltpu.VMEM((T,LT),f32)]*2,
        compiler_params=pltpu.CompilerParams(vmem_limit_bytes=48<<20))(x,par,skip)
def ema_bwd(g,m,x,par,skip,s0):
    T,W = x.shape
    return pl.pallas_call(bwd_kernel, out_shape=(jax.ShapeDtypeStruct((T,W),f32), jax.ShapeDtypeStruct((72,W),f32)),
        in_specs=[VM]*6, out_specs=(VM,VM), name="ema_bwd",
        scratch_shapes=[pltpu.VMEM((T//CH,CH,LT),f32), pltpu.VMEM((T//CH+1,HD,CH,LT),f32)]+[pltpu.VMEM((T,LT),f32)]*3,
        compiler_params=pltpu.CompilerParams(vmem_limit_bytes=48<<20))(g,m,x,par,skip,s0)


def tile(loc, rem, q, rel, s):
    return loc[q ^ rel] if s == 0 else rem[rel][s - 1]


def value_kernel(idx, n0, n1, o0, o1, loc, r0, r1, r2, r3, full, pre, val):
    z, q, c, x = idx[0], idx[1], idx[2], idx[3]
    rem = (r0, r1, r2, r3)
    full[:, at(2 * c + x, 256)] = n0[...]
    full[:, at(2 * c + 1 - x, 256)] = n1[...]
    full[:, at(2 - 2 * c + x, 256)] = o0[...]
    full[:, at(3 - 2 * c - x, 256)] = o1[...]
    for s in range(4):
        acc = None
        for rel in range(4):
            t = dot(full[:, at(q ^ rel, 256)], tile(loc, rem, q, rel, s))
            acc = t if acc is None else acc + t
        v = at(lax.rem(z + 4 - s, 4), 256)
        pre[:, v] = acc
        val[:, v] = silu(acc).astype(bf16)


def proj_kernel(
    idx, n0, n1, o0, o1, loc, r0, r1, r2, r3, wsl, ws1, ws2, ws3, aff,
    full, reset, update, hidden, shp, qs, ks,
):
    z, q, c, x = idx[0], idx[1], idx[2], idx[3]
    rem = (r0, r1, r2, r3)
    full[:, at(2 * c + x, 256)] = n0[...]
    full[:, at(2 * c + 1 - x, 256)] = n1[...]
    full[:, at(2 - 2 * c + x, 256)] = o0[...]
    full[:, at(3 - 2 * c - x, 256)] = o1[...]
    rows = [full[:, at(lax.rem(z + 4 - s, 4), 256)] for s in range(4)]
    acc = None
    for s, w in enumerate((wsl, ws1, ws2, ws3)):
        t = dot(rows[s], w[...])
        acc = t if acc is None else acc + t
    shp[...] = acc
    sh = silu(acc)
    qs[...] = (sh * aff[0:1, :] + aff[1:2, :]).astype(bf16)
    ks[...] = (sh * aff[2:3, :]).astype(bf16)
    for rel in range(4):
        acc = None
        for s in range(4):
            t = dot(rows[s], tile(loc, rem, q, rel, s))
            acc = t if acc is None else acc + t
        b = q ^ rel
        reset[:, at(b, 256)] = acc[:, 0:256]
        update[:, at(b, 128)] = acc[:, 256:384]
        hidden[:, at(b, 128)] = acc[:, 384:512]


def attend_kernel(
    idx, qs, ko, kn, vo, vn, reset, loc, r0, r1, r2, r3, probs, att, gated, own, send, part,
):
    z, q, c, x = idx[0], idx[1], idx[2], idx[3]
    rem = (r0, r1, r2, r3)
    t = qs.shape[0]
    scale = qs.shape[1] ** (-0.5)
    tm = 256
    for i in range(t // tm):
        r = slice(i * tm, (i + 1) * tm)
        row = x * t + i * tm + lax.broadcasted_iota(jnp.int32, (tm, t), 0)
        parts = []
        for k, half in ((ko, x), (kn, 1 - x)):
            col = half * t + lax.broadcasted_iota(jnp.int32, (tm, t), 1)
            seen = col <= row
            for n in range(2):
                first = idx[4 + n]
                lo = jnp.minimum(row, col) >= first
                hi = jnp.maximum(row, col) < first + PIECE
                seen = seen | (lo & hi)
            parts.append(jnp.where(seen, dot_t(qs[r, :], k[...]) * scale, -1e30))
        top = jnp.maximum(
            jnp.max(parts[0], axis=1, keepdims=True), jnp.max(parts[1], axis=1, keepdims=True)
        )
        e = [jnp.exp(p - top) for p in parts]
        total = jnp.sum(e[0], axis=1, keepdims=True) + jnp.sum(e[1], axis=1, keepdims=True)
        inv = 1.0 / total
        p = [(v * inv).astype(bf16) for v in e]
        probs[r, 0:t] = p[0]
        probs[r, t : 2 * t] = p[1]
        a = dot(p[0], vo[...]) + dot(p[1], vn[...])
        att[r, :] = a
        gated[r, :] = (silu(reset[r, :]) * a).astype(bf16)
    for rel in range(4):
        acc = None
        for s in range(4):
            v = dot(gated[:, at(lax.rem(z + 4 - s, 4), 256)], tile(loc, rem, q, rel, s))
            acc = v if acc is None else acc + v
        part[:, at(q ^ rel, 256)] = acc
    own[...] = part[:, at(c, 512)]
    send[...] = part[:, at(1 - c, 512)].astype(bf16)


def state_kernel(idx, hidden, own, recv, upd, xs, hpre, state, st):
    h = hidden[...] + own[...] + recv[...].astype(f32)
    hpre[...] = h
    u = sig(upd[...])
    v = u * silu(h) + (1.0 - u) * xs[...]
    state[...] = v
    mean = jnp.mean(v, axis=1, keepdims=True)
    second = jnp.sum(jnp.square(v - mean), axis=1, keepdims=True)
    lane = lax.broadcasted_iota(jnp.int32, st.shape, 1)
    st[...] = jnp.where(lane < 64, mean, second)


def unit_of(state, st, so):
    w = state.shape[1]
    m0, m1 = st[:, 0:1], so[:, 0:1]
    mean = 0.5 * (m0 + m1)
    total = st[:, 64:65] + so[:, 64:65] + w * (jnp.square(m0 - mean) + jnp.square(m1 - mean))
    inv = lax.rsqrt(total / (2 * w) + EPS)
    return (state[...] - mean) * inv, inv


def unit_kernel(idx, state, st, so, gain, low):
    unit, _ = unit_of(state, st, so)
    low[...] = (unit * gain[...]).astype(bf16)


def join(full, a, b, c):
    w = a.shape[1]
    full[:, at(c, w)] = a[...]
    full[:, at(1 - c, w)] = b[...]


def ffn_kernel(
    idx, s0, s1, g0, g1, il, i0, i1, i2, i3, ol, o0, o1, o2, o3,
    sf, gf, low, gffn, own, send, part,
):
    q, c = idx[1], idx[2]
    ri, ro = (i0, i1, i2, i3), (o0, o1, o2, o3)
    join(sf, s0, s1, c)
    join(gf, g0, g1, c)
    for s in range(4):
        f = slice(s * 512, (s + 1) * 512)
        pre = None
        for rel in range(4):
            t = dot(sf[:, at(q ^ rel, 256)], tile(il, ri, q, rel, s))
            pre = t if pre is None else pre + t
        low[:, f] = silu(pre).astype(bf16)
        g = None
        for rel in range(4):
            t = dot_t(gf[:, at(q ^ rel, 256)], tile(ol, ro, q, rel, s))
            g = t if g is None else g + t
        gffn[:, f] = (g * silu_grad(pre)).astype(bf16)
    for rel in range(4):
        acc = None
        for s in range(4):
            t = dot_t(gffn[:, s * 512 : (s + 1) * 512], tile(il, ri, q, rel, s))
            acc = t if acc is None else acc + t
        part[:, at(q ^ rel, 256)] = acc
    own[...] = part[:, at(c, 512)]
    send[...] = part[:, at(1 - c, 512)].astype(bf16)


def branch_kernel(idx, low, ol, o0, o1, o2, o3, own, send, part):
    q, c = idx[1], idx[2]
    ro = (o0, o1, o2, o3)
    for rel in range(4):
        acc = None
        for s in range(4):
            t = dot(low[:, s * 512 : (s + 1) * 512], tile(ol, ro, q, rel, s))
            acc = t if acc is None else acc + t
        part[:, at(q ^ rel, 256)] = acc
    own[...] = part[:, at(c, 512)]
    send[...] = part[:, at(1 - c, 512)].astype(bf16)


def grad_out_kernel(idx, low, gf, *outs):
    q = idx[1]
    n = outs[0].shape[1]
    for s in range(4):
        a = low[:, s * n : (s + 1) * n]
        for rel in range(4):
            outs[rel][s] = t_dot(a, gf[:, at(q ^ rel, 256)]).astype(bf16)


def grad_in_kernel(idx, sf, gffn, *outs):
    q = idx[1]
    n = outs[0].shape[2]
    for rel in range(4):
        a = sf[:, at(q ^ rel, 256)]
        for s in range(4):
            outs[rel][s] = t_dot(a, gffn[:, s * n : (s + 1) * n]).astype(bf16)


def grad_unit_kernel(idx, own, recv, state, st, so, gain, gu, st2, gno):
    unit, _ = unit_of(state, st, so)
    g = own[...] + recv[...].astype(f32)
    gu[...] = g
    gno[...] = jnp.sum(g * unit, axis=0, keepdims=True)
    gn = g * gain[...]
    lane = lax.broadcasted_iota(jnp.int32, st2.shape, 1)
    st2[...] = jnp.where(
        lane < 64, jnp.sum(gn, axis=1, keepdims=True), jnp.sum(gn * unit, axis=1, keepdims=True)
    )


def grad_state_kernel(idx, gu, state, st, so, t0, t1, gain, cot, hpre, upd, xs, ug, hg, gi):
    unit, inv = unit_of(state, st, so)
    d = 2 * state.shape[1]
    m1 = (t0[:, 0:1] + t1[:, 0:1]) / d
    m2 = (t0[:, 64:65] + t1[:, 64:65]) / d
    gs = cot[...] + inv * (gu[...] * gain[...] - m1 - unit * m2)
    u = sig(upd[...])
    h = hpre[...]
    s = sig(h)
    ug[...] = (gs * (h * s - xs[...]) * u * (1.0 - u)).astype(bf16)
    hg[...] = (gs * u * (s * (1.0 + h * (1.0 - s)))).astype(bf16)
    gi[...] = gs * (1.0 - u)


def gate_kernel(
    idx, h0, h1, ug, reset, att, probs, loc, r0, r1, r2, r3, hf, cat, gatt, vsend, gr,
):
    z, q, c = idx[0], idx[1], idx[2]
    rem = (r0, r1, r2, r3)
    t = h0.shape[0]
    join(hf, h0, h1, c)
    for s in range(4):
        v = at(lax.rem(z + 4 - s, 4), 256)
        g = None
        for rel in range(4):
            w = dot_t(hf[:, at(q ^ rel, 256)], tile(loc, rem, q, rel, s))
            g = w if g is None else g + w
        r = reset[:, v]
        sg = sig(r)
        gatt[:, v] = (g * (r * sg)).astype(bf16)
        gr[:, v] = (g * att[:, v] * (sg * (1.0 + r * (1.0 - sg)))).astype(bf16)
    for rel in range(4):
        b = q ^ rel
        cat[rel, :, 0:256] = gr[:, at(b, 256)]
        cat[rel, :, 256:384] = ug[:, at(b, 128)]
        cat[rel, :, 384:512] = h0[:, at(b, 128)]
    vsend[...] = t_dot(probs[:, t : 2 * t], gatt[...]).astype(bf16)


def attend_back_kernel(idx, probs, gatt, vo, vn, ko, kn, qs, qg, kown, ksend, vown):
    t = qs.shape[0]
    scale = qs.shape[1] ** (-0.5)
    p = [probs[:, 0:t].astype(f32), probs[:, t : 2 * t].astype(f32)]
    g = [dot_t(gatt[...], vo[...]), dot_t(gatt[...], vn[...])]
    center = jnp.sum(p[0] * g[0], axis=1, keepdims=True) + jnp.sum(p[1] * g[1], axis=1, keepdims=True)
    gs = [(a * (b - center) * scale).astype(bf16) for a, b in zip(p, g)]
    ksend[...] = t_dot(gs[1], qs[...]).astype(bf16)
    qg[...] = dot(gs[0], ko[...]) + dot(gs[1], kn[...])
    kown[...] = t_dot(gs[0], qs[...])
    vown[...] = t_dot(probs[:, 0:t], gatt[...])


def value_back_kernel(idx, vown, vrecv, pre, loc, r0, r1, r2, r3, gv, own, send, part):
    z, q, c = idx[0], idx[1], idx[2]
    rem = (r0, r1, r2, r3)
    gv[...] = ((vown[...] + vrecv[...].astype(f32)) * silu_grad(pre[...])).astype(bf16)
    for rel in range(4):
        acc = None
        for s in range(4):
            w = dot_t(gv[:, at(lax.rem(z + 4 - s, 4), 256)], tile(loc, rem, q, rel, s))
            acc = w if acc is None else acc + w
        part[:, at(q ^ rel, 256)] = acc
    own[...] = part[:, at(c, 512)]
    send[...] = part[:, at(1 - c, 512)].astype(bf16)


def mixer_back_kernel(
    idx, cat, loc, r0, r1, r2, r3, wsl, ws1, ws2, ws3, aff, shp, qg, kown, krecv, gs, ga, own, send, part,
):
    z, q, c = idx[0], idx[1], idx[2]
    rem = (r0, r1, r2, r3)
    kg = kown[...] + krecv[...].astype(f32)
    s_pre = shp[...]
    sh = silu(s_pre)
    g = qg[...]
    gs[...] = ((g * aff[0:1, :] + kg * aff[2:3, :]) * silu_grad(s_pre)).astype(bf16)
    ga[0:1, :] = jnp.sum(g * sh, axis=0, keepdims=True)
    ga[1:2, :] = jnp.sum(g, axis=0, keepdims=True)
    ga[2:3, :] = jnp.sum(kg * sh, axis=0, keepdims=True)
    for s, w in enumerate((wsl, ws1, ws2, ws3)):
        acc = dot_t(gs[...], w[...])
        for rel in range(4):
            acc = acc + dot_t(cat[rel], tile(loc, rem, q, rel, s))
        part[:, at(lax.rem(z + 4 - s, 4), 256)] = acc
    own[...] = part[:, at(c, 512)]
    send[...] = part[:, at(1 - c, 512)].astype(bf16)


def grad_pack_kernel(idx, mf, cat, *outs):
    z = idx[0]
    for s in range(4):
        a = mf[:, at(lax.rem(z + 4 - s, 4), 256)]
        for rel in range(4):
            outs[rel][s] = t_dot(a, cat[rel]).astype(bf16)


def grad_u_kernel(idx, gated, hf, *outs):
    z, q = idx[0], idx[1]
    for s in range(4):
        a = gated[:, at(lax.rem(z + 4 - s, 4), 256)]
        for rel in range(4):
            outs[rel][s] = t_dot(a, hf[:, at(q ^ rel, 256)]).astype(bf16)


def grad_value_kernel(idx, nf, gv, mf, gs, o0, o1, o2, o3, gws):
    z, q = idx[0], idx[1]
    outs = (o0, o1, o2, o3)
    for rel in range(4):
        a = nf[:, at(q ^ rel, 256)]
        for s in range(4):
            outs[rel][s] = t_dot(a, gv[:, at(lax.rem(z + 4 - s, 4), 256)]).astype(bf16)
    gws[...] = t_dot(mf[...], gs[...])


def place(k):
    return [
        ((x * 2 + c) * 4 + z, (((z + k) % 2) * 2 + z // 2) * 4 + 2 * x + c)
        for x in range(2)
        for c in range(2)
        for z in range(4)
    ]


def pick(pred, a, b, axis):
    return jnp.where(pred, jnp.concatenate([a, b], axis), jnp.concatenate([b, a], axis))


def to_chips(a):
    z = lax.axis_index("tensor")
    halves = a.reshape(2, a.shape[0] // 2, a.shape[1])
    return [
        lax.ppermute(lax.dynamic_index_in_dim(halves, (z + k) % 2, 0, False), GROUP, place(k))
        for k in range(2)
    ]


def from_chips(a):
    z = lax.axis_index("tensor")
    x = lax.axis_index("xx")
    w = a.shape[1] // 2
    r = [
        lax.ppermute(
            lax.dynamic_slice_in_dim(a, ((x + k) % 2) * w, w, 1),
            GROUP,
            [(t, s) for s, t in place(k)],
        )
        for k in range(2)
    ]
    return pick(z % 2 == 0, r[0], r[1], 0)


def swap2(a, axis):
    return lax.ppermute(a, axis, [(0, 1), (1, 0)])


def shifted(a, axis, count, s):
    return lax.ppermute(a, axis, [(i, (i + s) % count) for i in range(count)])


def moments(rows, axis, count):
    width = rows.shape[1]
    mean = jnp.mean(rows, axis=1)
    second = jnp.sum(jnp.square(rows - mean[:, None]), axis=1)
    both = jnp.stack([mean, second])
    parts = [both] + [shifted(both, axis, count, s) for s in range(1, count)]
    total_mean = sum(p[0] for p in parts) / count
    total = sum(p[1] + width * jnp.square(p[0] - total_mean) for p in parts)
    return total_mean[:, None], lax.rsqrt(total / (width * count) + EPS)[:, None]


def sum_over(v, axis, count):
    return v + sum(shifted(v, axis, count, s) for s in range(1, count))


def sum_devices(v, rest, axes):
    for a in axes:
        v = v + (swap2(v, a) if a != "tensor" else sum(shifted(v, a, 4, s) for s in range(1, 4)))
    return lax.psum(v, "rest") if rest > 1 else v


def gather(loc, q, x_first):
    mine = lax.dynamic_index_in_dim(loc, q, 0, False)
    three = jnp.stack([shifted(mine, "tensor", 4, s) for s in range(1, 4)])
    nx = swap2(three, "xx")
    ny = swap2(three, "yy")
    nxy = swap2(nx, "yy") if x_first else swap2(ny, "xx")
    return [three, nx, ny, nxy]


def add(a, b):
    return (a.astype(f32) + b.astype(f32)).astype(bf16)


def reduce_blocks(g, rest, x_first):
    if rest > 1:
        g = [lax.psum(v, "rest") for v in g]
    first, second, near, far = ("xx", "yy", 1, 2) if x_first else ("yy", "xx", 2, 1)
    own = add(g[0], swap2(g[near], first))
    side = add(g[far], swap2(g[3], first))
    own = add(own, swap2(side, second))
    total = own[0].astype(f32)
    for s in range(1, 4):
        total = total + shifted(own[s], "tensor", 4, 4 - s).astype(f32)
    return total


def on_device(
    inputs,
    norm_in,
    w_value,
    expand,
    ema_rate,
    damping,
    project,
    ema_skip,
    w_shared,
    qk_affine,
    w_reset,
    w_update,
    w_hidden,
    u_hidden,
    norm_out,
    w_in,
    w_out,
    cotangent,
    piece_starts,
):
    c = lax.axis_index("core")
    z = lax.axis_index("tensor")
    x = lax.axis_index("xx")
    q = lax.axis_index(PLANE)
    rest = lax.axis_size("rest")
    length, width = inputs.shape
    d = width * 4
    dh = d // 2
    t = length // 2

    def half(a, dim):
        n = a.shape[dim] // 2
        return lax.dynamic_slice_in_dim(a, c * n, n, dim)

    def by_rows(a):
        return a.reshape(4, a.shape[0] // 4, a.shape[1])

    def by_cols(a):
        n = a.shape[1] // 4
        return jnp.stack([a[:, i * n : (i + 1) * n] for i in range(4)])

    starts = lax.ppermute(piece_starts, GROUP, place(0))[0]
    idx = jnp.concatenate([jnp.stack([z, q, c, x]).astype(jnp.int32), starts])

    norm_in_own = lax.dynamic_slice_in_dim(norm_in, z * width, width, 0)
    mean_in, inv_in = moments(inputs, "tensor", 4)
    unit_in = (inputs - mean_in) * inv_in
    normed = unit_in * norm_in_own
    par = jnp.concatenate([expand.T, ema_rate.T, damping.T, project.T], 0)
    skip = ema_skip[None, :]
    nb = to_chips(normed.astype(bf16))
    mixed, mixer_low, s0 = ema_fwd(normed, par, skip)
    mb = to_chips(mixer_low)

    lv = by_rows(half(w_value, 1))
    k = w_reset.shape[0]
    vq = w_reset.shape[1] // 4
    wr4 = lax.dynamic_slice_in_dim(w_reset.reshape(k, 4, vq), c * (vq // 2), vq // 2, 2)
    lp = jnp.concatenate(
        [jnp.moveaxis(wr4, 1, 0), by_cols(half(w_update, 1)), by_cols(half(w_hidden, 1))], 2
    )
    lu = by_cols(half(u_hidden, 0))
    li = by_rows(half(w_in, 1))
    lo = by_cols(half(w_out, 0))
    wv = [lv] + gather(lv, q, True)
    wsh = [w_shared] + [shifted(w_shared, "tensor", 4, s) for s in range(1, 4)]
    wp = [lp] + gather(lp, q, False)
    wu = [lu] + gather(lu, q, True)
    wi = [li] + gather(li, q, False)
    wo = [lo] + gather(lo, q, True)

    x_sp = to_chips(inputs)
    x_sp = pick(x == 0, x_sp[0], x_sp[1], 1)
    cot = to_chips(cotangent)
    cot = pick(x == 0, cot[0], cot[1], 1)
    cot_low = cot.astype(bf16)
    cot_other = swap2(cot_low, "core")

    nf, value_pre, values = call(
        value_kernel,
        [shape((t, d), bf16), shape((t, d), f32), shape((t, d), bf16)],
        idx, *nb, *[swap2(b, "core") for b in nb], *wv, name="value",
    )
    values_n = swap2(values, "xx")
    mf, reset, update, hidden, shp, qs, ks = call(
        proj_kernel,
        [
            shape((t, d), bf16), shape((t, d), f32), shape((t, dh), f32), shape((t, dh), f32),
            shape((t, 128), f32), shape((t, 128), bf16), shape((t, 128), bf16),
        ],
        idx, *mb, *[swap2(b, "core") for b in mb], *wp, *wsh, qk_affine, name="proj",
    )
    ks_n = swap2(ks, "xx")
    probs, att, gated, own, send = call(
        attend_kernel,
        [
            shape((t, 2 * t), bf16), shape((t, d), f32), shape((t, d), bf16),
            shape((t, dh), f32), shape((t, dh), bf16),
        ],
        idx, qs, ks, ks_n, values, values_n, reset, *wu, name="attend",
        scratch=[pltpu.VMEM((t, d), f32)],
    )
    gain = lax.dynamic_slice_in_dim(norm_out, c * dh, dh, 0)[None, :]
    half_f = shape((t, dh), f32)
    half_b = shape((t, dh), bf16)
    stat = shape((t, 128), f32)
    hpre, state, st = call(
        state_kernel, [half_f, half_f, stat], idx, hidden, own, swap2(send, "core"), update, x_sp, name="state"
    )
    so = swap2(st, "core")
    (low,) = call(unit_kernel, [half_b], idx, state, st, so, gain, name="unit")

    sf, gf, ffn_low, gffn, own, send = call(
        ffn_kernel,
        [shape((t, d), bf16), shape((t, d), bf16), shape((t, 2 * d), bf16), shape((t, 2 * d), bf16), half_f, half_b],
        idx, low, swap2(low, "core"), cot_low, cot_other, *wi, *wo, name="ffn",
        scratch=[pltpu.VMEM((t, d), f32)],
    )
    gunit, st2, gno = call(
        grad_unit_kernel, [half_f, stat, shape((1, dh), f32)],
        idx, own, swap2(send, "core"), state, st, so, gain, name="grad_unit",
    )
    ug, hg, gi = call(
        grad_state_kernel, [half_b, half_b, half_f],
        idx, gunit, state, st, so, st2, swap2(st2, "core"), gain, cot, hpre, update, x_sp, name="grad_state",
    )
    gi_direct = from_chips(gi)
    own, send = call(
        branch_kernel, [half_f, half_b], idx, ffn_low, *wo, name="branch", scratch=[pltpu.VMEM((t, d), f32)]
    )
    outputs = from_chips(state + own + swap2(send, "core").astype(f32))

    def blocks(r, m):
        return [shape((4, r, m), bf16)] * 4

    g_wo = call(grad_out_kernel, blocks(512, 256), idx, ffn_low, gf, name="grad_w_out")
    g_wi = call(grad_in_kernel, blocks(256, 512), idx, sf, gffn, name="grad_w_in")
    r_wo = reduce_blocks(g_wo, rest, True)
    r_wi = reduce_blocks(g_wi, rest, False)

    hf, cat, gatt, vsend = call(
        gate_kernel,
        [shape((t, d), bf16), shape((4, t, 512), bf16), shape((t, d), bf16), shape((t, d), bf16)],
        idx, hg, swap2(hg, "core"), ug, reset, att, probs, *wu, name="gate",
        scratch=[pltpu.VMEM((t, d), bf16)],
    )
    vrecv = swap2(vsend, "xx")
    qg, kown, ksend, vown = call(
        attend_back_kernel,
        [shape((t, 128), f32), shape((t, 128), f32), shape((t, 128), bf16), shape((t, d), f32)],
        idx, probs, gatt, values, values_n, ks, ks_n, qs, name="attend_back",
    )
    g_uh = call(grad_u_kernel, blocks(256, 256), idx, gated, hf, name="grad_u_hidden")
    g_pk = call(grad_pack_kernel, blocks(256, 512), idx, mf, cat, name="grad_pack")
    r_uh = reduce_blocks(g_uh, rest, True)
    r_pk = reduce_blocks(g_pk, rest, False)
    gs, ga, own, send = call(
        mixer_back_kernel,
        [shape((t, 128), bf16), shape((3, 128), f32), half_f, half_b],
        idx, cat, *wp, *wsh, qk_affine, shp, qg, kown, swap2(ksend, "xx"), name="mixer_back",
        scratch=[pltpu.VMEM((t, d), f32)],
    )
    grad_mixer = from_chips((own + swap2(send, "core").astype(f32)).astype(bf16))
    gv, own, send = call(
        value_back_kernel, [shape((t, d), bf16), half_f, half_b],
        idx, vown, vrecv, value_pre, *wv, name="value_back", scratch=[pltpu.VMEM((t, d), f32)],
    )
    normed_part = from_chips((own + swap2(send, "core").astype(f32)).astype(bf16))
    *g_wv, g_ws = call(
        grad_value_kernel, blocks(256, 256) + [shape((d, 128), f32)], idx, nf, gv, mf, gs, name="grad_w_value"
    )
    r_wv = reduce_blocks(g_wv, rest, True)

    ema_grad, g_par = ema_bwd(grad_mixer, mixed, normed, par, skip, s0)
    grad_normed = normed_part.astype(f32) + ema_grad
    g_norm_in = jnp.sum(grad_normed * unit_in, axis=0)
    gn = grad_normed * norm_in_own
    sums = sum_over(jnp.stack([jnp.sum(gn, 1), jnp.sum(gn * unit_in, 1)]), "tensor", 4) / d
    grad_inputs = gi_direct + inv_in * (gn - sums[0][:, None] - unit_in * sums[1][:, None])

    near = ("core", "xx", "yy")
    small = sum_devices(jnp.concatenate([g_par, g_norm_in[None, :]], 0), rest, near)
    wide = jnp.concatenate(
        [lax.dynamic_update_slice(jnp.zeros((d,), f32), gno[0], (c * dh,)), ga.reshape(-1)]
    )
    wide = sum_devices(wide.reshape(-1, 128), rest, near + ("tensor",)).reshape(-1)
    gno = lax.dynamic_slice_in_dim(wide, z * width, width, 0)
    gaff = wide[d:].reshape(3, -1)

    g_ws = g_ws.astype(bf16).reshape(4, width, 128)
    part = lax.dynamic_index_in_dim(g_ws, z, 0, False).astype(f32)
    for s in range(1, 4):
        part = part + shifted(
            lax.dynamic_index_in_dim(g_ws, (z + s) % 4, 0, False), "tensor", 4, s
        ).astype(f32)
    part = sum_devices(part, rest, near)
    dp = rest * 8
    me = lax.axis_index(DPS)
    o_ws = lax.dynamic_slice_in_dim(part, me * (128 // dp), 128 // dp, 1)

    r = lax.axis_index("rest")

    def swap_join(g, dim, other):
        if rest > 1:
            n = g.shape[dim] // rest
            g = lax.dynamic_slice_in_dim(g, r * n, n, dim)
        n = g.shape[dim] // 2
        keep = lax.dynamic_slice_in_dim(g, c * n, n, dim)
        send = lax.dynamic_slice_in_dim(g, (1 - c) * n, n, dim)
        return pick(c == 0, keep, swap2(send, "core"), other)

    o_wv = swap_join(r_wv, 0, 1)
    o_wi = swap_join(r_wi, 0, 1)
    o_wo = swap_join(r_wo, 1, 0)
    o_uh = swap_join(r_uh, 1, 0)
    o_wr, both = r_pk[:, 0:256], r_pk[:, 256:512]
    if rest > 1:
        n = o_wr.shape[1] // rest
        o_wr = lax.all_gather(o_wr, "core", axis=1, tiled=True)
        o_wr = lax.dynamic_slice_in_dim(o_wr, (r * 2 + c) * n, n, 1)
        pair = [lax.all_gather(v, ("core",) + PLANE, axis=1, tiled=True) for v in (both[:, 0:128], both[:, 128:256])]
        o_wu, o_wh = [lax.dynamic_slice_in_dim(v, me * (d // dp), d // dp, 1) for v in pair]
    else:
        both = lax.ppermute(both, PLANE + ("core",), [(b % 4 * 2 + b // 4, b) for b in range(8)])
        o_wu, o_wh = both[:, 0:128], both[:, 128:256]
    return (
        outputs,
        grad_inputs,
        small[72],
        o_wv,
        small[0:16].T,
        small[16:32].T,
        small[32:48].T,
        small[48:64].T,
        small[64],
        o_ws,
        gaff,
        o_wr,
        o_wu,
        o_wh,
        o_uh,
        gno,
        o_wi,
        o_wo,
    )


def solution(mesh):
    devices = np.asarray(mesh.devices)
    dp, tensor = devices.shape
    inner = Mesh(devices.reshape(2, 2, dp // 8, 2, tensor), ALL)
    t = "tensor"
    placed = (
        P(DPS, t),
        P(),
        P(None, t),
        P(t, None),
        P(t, None),
        P(t, None),
        P(t, None),
        P(t),
        P(t, None),
        P(),
        P(t, None),
        P(t, None),
        P(t, None),
        P(t, None),
        P(),
        P(None, t),
        P(t, None),
        P(DPS, t),
        P(DPS, None),
    )
    return jax.shard_map(
        on_device,
        mesh=inner,
        in_specs=placed,
        out_specs=(
            P(DPS, t),
            P(DPS, t),
            P(t),
            P(DPS, t),
            P(t, None),
            P(t, None),
            P(t, None),
            P(t, None),
            P(t),
            P(t, DPS),
            P(),
            P(t, DPS),
            P(t, DPS),
            P(t, DPS),
            P(t, DPS),
            P(t),
            P(DPS, t),
            P(t, DPS),
        ),
        check_vma=False,
    )
```

time: 1390 us -> 775 us (0.56)
  waiting for transfers between devices: 891 us -> 379 us
  matrix products: 197 us -> 0 us
  starting transfers between devices: 2.32 us -> 174 us
  Pallas kernels: 0 us -> 106 us
  other arithmetic: 115 us -> 38.1 us
  blocking collectives: 57.1 us -> 0 us
  local copies, waits for them, and re-layouts: 98.1 us -> 65.8 us
    reduce_scatter x15 -> x0, waiting for transfers between devices: 576 us -> none  [the longest x1 132 us: on_device(): lax.psum_scatter(jnp.dot(mixer_low, w_reset, preferred_element_type=jnp.f...]
    ppermute x0 -> x124, waiting for transfers between devices: none -> 379 us  [the longest x61 183 us: swap2(): return lax.ppermute(a, axis, [(0, 1), (1, 0)])]
    all_gather x6 -> x0, waiting for transfers between devices: 279 us -> none  [the longest x1 78.5 us: on_device(): lax.all_gather(reset_grad_low, 'tensor', axis=1, tiled=True)]
    dot_general x47 -> x0, matrix products: 197 us -> none  [the longest x3 43.3 us: ema_mix(): in_block = jnp.einsum('ijc,njc->nic', toeplitz, blocks, precision=highest)]
    ppermute x0 -> x124, starting transfers between devices: none -> 174 us  [the longest x61 71 us: swap2(): return lax.ppermute(a, axis, [(0, 1), (1, 0)])]
    pallas_call x0 -> x20, Pallas kernels: none -> 106 us  [the longest x18 86 us: call(): pl.pallas_call(body, out_shape=tuple(outs), in_specs=[SM] + [VM] * len(ar...]
    psum x2 -> x0, blocking collectives: 40 us -> none  [the longest x1 22.4 us: on_device(): lax.psum((grad_norm_in, grad_expand, grad_ema_rate, grad_damping, grad_pr...]
    psum x1 -> x0, waiting for transfers between devices: 34.5 us -> none  [on_device(): lax.psum(shared_part.astype(jnp.bfloat16), 'tensor').astype(jnp.float32)]
  transfers between devices with their start and end apart: 22 -> 124, of which waited for: 17 -> 53; matrix products, arithmetic and copies ran while one was open for 23% -> 8% of each run, Pallas kernels for 0% -> 11%
where the time goes in v1:
time: 775 us; the launch traced here: 765 us
  waiting for transfers between devices  379 us (49%)
  starting transfers between devices  174 us (22%)
  Pallas kernels  106 us (14%)
  local copies, waits for them, and re-layouts  65.8 us (8%)
  other arithmetic  38.1 us (5%)
    ppermute x61, waiting for transfers between devices, swap2(): return lax.ppermute(a, axis, [(0, 1), (1, 0)])  183 us
    ppermute x45, waiting for transfers between devices, shifted(): return lax.ppermute(a, axis, [(i, (i + s) % count) for i in range(count)])  118 us
    pallas_call x18, Pallas kernels, call(): pl.pallas_call(body, out_shape=tuple(outs), in_specs=[SM] + [VM] * len(ar...  86 us
    ppermute x61, starting transfers between devices, swap2(): return lax.ppermute(a, axis, [(0, 1), (1, 0)])  71 us
    ppermute x45, starting transfers between devices, shifted(): return lax.ppermute(a, axis, [(i, (i + s) % count) for i in range(count)])  62.3 us
    unnamed x331, local copies, waits for them, and re-layouts  41.1 us
    ppermute x8, waiting for transfers between devices, from_chips(): lax.ppermute(lax.dynamic_slice_in_dim(a, (x + k) % 2 * w, w, 1), GROUP, [...  34.3 us
    ppermute x8, waiting for transfers between devices, to_chips(): lax.ppermute(lax.dynamic_index_in_dim(halves, (z + k) % 2, 0, False), GRO...  33.1 us
  transfers between devices with their start and end apart: 124, of which 53 were waited for; matrix products, arithmetic and copies ran while one was open for 8% of the time, Pallas kernels for 11%

profile of v1, /device:TPU:10, one launch (start us, length us, event | category | flops | bytes accessed | tf_op | source)
XLA Modules:
  0.0 765.0 jit_solution(17373480878057734824)
XLA Ops:
  50.5 14.1 %collective-permute-done.24 = bf16[256,256]{1,0:T(8,128)(2,1)S(1)} collective-permute-done((bf16[256,256]{1,0:T(8,128)(2,1)}, bf16[256,256]{1,0:T(8,128)(2,1)S(1)}, u32[]{:S(2)}, u32[]{:S(2)}) %collective-permute-start.24) | collective-permute-done | bytes 131104 | tf_op jit(solution)/shard_map/ppermute | solution.py:570
  68.6 18.5 %collective-permute-done.31 = bf16[256,256]{1,0:T(8,128)(2,1)S(1)} collective-permute-done((bf16[256,256]{1,0:T(8,128)(2,1)S(1)}, bf16[256,256]{1,0:T(8,128)(2,1)S(1)}, u32[]{:S(2)}, u32[]{:S(2)}) %collective-permute-start.31) | collective-permute-done | bytes 131104 | tf_op jit(solution)/shard_map/ppermute | solution.py:570
  95.2 10.0 %collective-permute-done.50 = bf16[512,256]{1,0:T(8,128)(2,1)S(1)} collective-permute-done((bf16[512,256]{1,0:T(8,128)(2,1)}, bf16[512,256]{1,0:T(8,128)(2,1)S(1)}, u32[]{:S(2)}, u32[]{:S(2)}) %collective-permute-start.50) | collective-permute-done | bytes 262176 | tf_op jit(solution)/shard_map/ppermute | solution.py:570
  106.7 6.5 collective-permute-done.51
  121.2 6.4 collective-permute-done.18.n0
  135.3 5.5 ema_fwd.1
  164.8 5.6 collective-permute-done.4.n0
  181.4 29.2 %collective-permute-done.11.r1 = bf16[3,256,512]{2,1,0:T(8,128)(2,1)S(1)} collective-permute-done((bf16[3,256,512]{2,1,0:T(8,128)(2,1)S(1)}, bf16[3,256,512]{2,1,0:T(8,128)(2,1)S(1)}, u32[]{:S(2)}, u32[]{:S(2)}) %collective-permute-start.11) | collective-permute-done | bytes 786464 | tf_op jit(solution)/shard_map/ppermute | solution.py:566
  212.7 20.3 %collective-permute-done.13.r3 = bf16[3,256,512]{2,1,0:T(8,128)(2,1)S(1)} collective-permute-done((bf16[3,256,512]{2,1,0:T(8,128)(2,1)}, bf16[3,256,512]{2,1,0:T(8,128)(2,1)S(1)}, u32[]{:S(2)}, u32[]{:S(2)}) %collective-permute-start.13) | collective-permute-done | bytes 786464 | tf_op jit(solution)/shard_map/ppermute | solution.py:566
  233.7 6.5 proj.1
  240.3 6.7 collective-permute-start.45
  254.0 7.8 %attend.1 = (bf16[512,1024]{1,0:T(8,128)(2,1)S(1)}, f32[512,1024]{1,0:T(8,128)}, bf16[512,1024]{1,0:T(8,128)(2,1)S(1)}, f32[512,512]{1,0:T(8,128)S(1)}, bf16[512,512]{1,0:T(8,128)(2,1)}) custom-call(s32[6]{0:T(128)S(1)} %concatenate.75.idx, bf16[512,128]{1,0:T(8,128)(2,1)S(1)} %get-tuple-element.93.qs, bf16[512,128]{1,0:T(8,128)(2,1)S(1)} %get-tuple-element.94.ko, ...), custom_call_target="tpu_custom_call" | custom-call | tf_op jit(solution)/shard_map/attend/pallas_call | solution.py:31
  268.0 22.9 %collective-permute-start.52 = (bf16[3,512,256]{2,1,0:T(8,128)(2,1)}, bf16[3,512,256]{2,1,0:T(8,128)(2,1)}, u32[]{:S(2)}, u32[]{:S(2)}) collective-permute-start(bf16[3,512,256]{2,1,0:T(8,128)(2,1)} %pad_maximum_fusion.3.o0), channel_id=1, source_target_pairs={{0,8},{8,0},{1,9},{9,1},{2,10},{10,2},{3,11},{11,3},{4,12},{12,4},... | collective-permute-start | bytes 2359304 | tf_op jit(solution)/shard_map/ppermute | solution.py:566
  296.4 11.2 %collective-permute-done.41 = f32[512,256]{1,0:T(8,128)} collective-permute-done((f32[512,256]{1,0:T(8,128)}, f32[512,256]{1,0:T(8,128)}, u32[]{:S(2)}, u32[]{:S(2)}) %collective-permute-start.41) | collective-permute-done | bytes 524320 | tf_op jit(solution)/shard_map/ppermute | solution.py:545
  322.1 15.4 %collective-permute-done.53.o2 = bf16[3,512,256]{2,1,0:T(8,128)(2,1)S(1)} collective-permute-done((bf16[3,512,256]{2,1,0:T(8,128)(2,1)}, bf16[3,512,256]{2,1,0:T(8,128)(2,1)S(1)}, u32[]{:S(2)}, u32[]{:S(2)}) %collective-permute-start.53) | collective-permute-done | bytes 786464 | tf_op jit(solution)/shard_map/ppermute | solution.py:566
  338.1 15.8 %collective-permute-done.54.o3 = bf16[3,512,256]{2,1,0:T(8,128)(2,1)S(1)} collective-permute-done((bf16[3,512,256]{2,1,0:T(8,128)(2,1)}, bf16[3,512,256]{2,1,0:T(8,128)(2,1)S(1)}, u32[]{:S(2)}, u32[]{:S(2)}) %collective-permute-start.54) | collective-permute-done | bytes 786464 | tf_op jit(solution)/shard_map/ppermute | solution.py:566
  354.8 12.0 %ffn.1 = (bf16[512,1024]{1,0:T(8,128)(2,1)}, bf16[512,1024]{1,0:T(8,128)(2,1)}, bf16[512,2048]{1,0:T(8,128)(2,1)}, bf16[512,2048]{1,0:T(8,128)(2,1)}, f32[512,512]{1,0:T(8,128)}, /*index=5*/bf16[512,512]{1,0:T(8,128)(2,1)S(1)}) custom-call(s32[6]{0:T(128)S(1)} %concatenate.75.idx, bf16[512,512]{1,0:T(8,128)(2,1)S(1)} %unit.1.s0, ...), custom_call_target="tpu_custom_call" | custom-call | tf_op jit(solution)/shard_map/ffn/pallas_call | solution.py:31
  379.7 5.3 branch.1
  394.8 5.5 grad_w_in.1
  404.6 7.7 %gate.1 = (bf16[512,1024]{1,0:T(8,128)(2,1)S(1)}, bf16[4,512,512]{2,1,0:T(8,128)(2,1)}, bf16[512,1024]{1,0:T(8,128)(2,1)S(1)}, bf16[512,1024]{1,0:T(8,128)(2,1)}) custom-call(s32[6]{0:T(128)S(1)} %concatenate.75.idx, bf16[512,512]{1,0:T(8,128)(2,1)} %get-tuple-element.112.h0, bf16[512,512]{1,0:T(8,128)(2,1)} %collective-permute-done.62.h1, ...), custom_call_target="tpu_custom_call" | custom-call | tf_op jit(solution)/shard_map/gate/pallas_call | solution.py:31
  441.6 12.7 %collective-permute-done.91 = f32[11,128]{1,0:T(8,128)S(1)} collective-permute-done((f32[11,128]{1,0:T(8,128)S(1)}, f32[11,128]{1,0:T(8,128)S(1)}, u32[]{:S(2)}, u32[]{:S(2)}) %collective-permute-start.91) | collective-permute-done | bytes 5664 | tf_op jit(solution)/shard_map/ppermute | solution.py:566
  484.2 10.1 %collective-permute-done.104 = bf16[4,256,256]{2,1,0:T(8,128)(2,1)S(1)} collective-permute-done((bf16[4,256,256]{2,1,0:T(8,128)(2,1)S(1)}, bf16[4,256,256]{2,1,0:T(8,128)(2,1)S(1)}, u32[]{:S(2)}, u32[]{:S(2)}) %collective-permute-start.104) | collective-permute-done | bytes 524320 | tf_op jit(solution)/shard_map/ppermute | solution.py:566
  501.6 19.5 %collective-permute-done.110 = bf16[4,256,512]{2,1,0:T(8,128)(2,1)S(1)} collective-permute-done((bf16[4,256,512]{2,1,0:T(8,128)(2,1)S(1)}, bf16[4,256,512]{2,1,0:T(8,128)(2,1)S(1)}, u32[]{:S(2)}, u32[]{:S(2)}) %collective-permute-start.110) | collective-permute-done | bytes 1048608 | tf_op jit(solution)/shard_map/ppermute | solution.py:566
  527.0 24.0 %collective-permute-done.69 = bf16[512,256]{1,0:T(8,128)(2,1)S(1)} collective-permute-done((bf16[512,256]{1,0:T(8,128)(2,1)S(1)}, bf16[512,256]{1,0:T(8,128)(2,1)S(1)}, u32[]{:S(2)}, u32[]{:S(2)}) %collective-permute-start.69) | collective-permute-done | bytes 262176 | tf_op jit(solution)/shard_map/ppermute | solution.py:555
  552.2 14.3 %ema_bwd.1 = (f32[1024,256]{1,0:T(8,128)S(1)}, f32[72,256]{1,0:T(8,128)S(1)}) custom-call(bf16[1024,256]{1,0:T(8,128)(2,1)S(1)} %maximum_select_fusion.5.g_ref, f32[1024,256]{1,0:T(8,128)S(1)} %copy-done.44, f32[1024,256]{1,0:T(8,128)S(1)} %get-tuple-element.170.x_ref, f32[64,256]{1,0:T(8,128)S(1)} %pad_maximum_fusion.8.par_ref, f32[1,256]{1,0:T(1,128)S(1)} %bitcast.197, ...), custom_call_target="tpu_custom_call" | custom-call | tf_op jit(solution)/shard_map/ema_bwd/pallas_call | solution.py:209
  589.0 9.7 %collective-permute-done.122 = bf16[512,256]{1,0:T(8,128)(2,1)} collective-permute-done((bf16[512,256]{1,0:T(8,128)(2,1)}, bf16[512,256]{1,0:T(8,128)(2,1)}, u32[]{:S(2)}, u32[]{:S(2)}) %collective-permute-start.122) | collective-permute-done | bytes 262176 | tf_op jit(solution)/shard_map/ppermute | solution.py:570
  646.6 19.4 %collective-permute-done.78 = bf16[4,256,256]{2,1,0:T(8,128)(2,1)S(1)} collective-permute-done((bf16[4,256,256]{2,1,0:T(8,128)(2,1)S(1)}, bf16[4,256,256]{2,1,0:T(8,128)(2,1)S(1)}, u32[]{:S(2)}, u32[]{:S(2)}) %collective-permute-start.78) | collective-permute-done | bytes 524320 | tf_op jit(solution)/shard_map/ppermute | solution.py:566
  681.1 20.3 %collective-permute-done.75 = f32[73,256]{1,0:T(8,128)S(1)} collective-permute-done((f32[73,256]{1,0:T(8,128)S(1)}, f32[73,256]{1,0:T(8,128)S(1)}, u32[]{:S(2)}, u32[]{:S(2)}) %collective-permute-start.75) | collective-permute-done | bytes 74784 | tf_op jit(solution)/shard_map/ppermute | solution.py:566
  707.9 8.7 %collective-permute-done.76 = f32[73,256]{1,0:T(8,128)S(1)} collective-permute-done((f32[73,256]{1,0:T(8,128)S(1)}, f32[73,256]{1,0:T(8,128)S(1)}, u32[]{:S(2)}, u32[]{:S(2)}) %collective-permute-start.76) | collective-permute-done | bytes 74784 | tf_op jit(solution)/shard_map/ppermute | solution.py:566
  724.8 14.0 %collective-permute-done.80 = bf16[256,256]{1,0:T(8,128)(2,1)S(1)} collective-permute-done((bf16[256,256]{1,0:T(8,128)(2,1)S(1)}, bf16[256,256]{1,0:T(8,128)(2,1)S(1)}, u32[]{:S(2)}, u32[]{:S(2)}) %collective-permute-start.80) | collective-permute-done | bytes 131104 | tf_op jit(solution)/shard_map/ppermute | solution.py:570
  739.0 7.4 collective-permute-done.100
  755.9 8.2 %collective-permute-done.102 = f32[256,256]{1,0:T(8,128)S(1)} collective-permute-done((f32[256,256]{1,0:T(8,128)S(1)}, f32[256,256]{1,0:T(8,128)S(1)}, u32[]{:S(2)}, u32[]{:S(2)}) %collective-permute-start.102) | collective-permute-done | bytes 262176 | tf_op jit(solution)/shard_map/ppermute | solution.py:844
  (673 shorter events, 361.0 us)
Async XLA Ops:
  42.6 44.4 %collective-permute-start.8 = (bf16[256,512]{1,0:T(8,128)(2,1)}, bf16[256,512]{1,0:T(8,128)(2,1)S(1)}, u32[]{:S(2)}, u32[]{:S(2)}) collective-permute-start(bf16[256,512]{1,0:T(8,128)(2,1)} %dynamic-slice_bitcast_fusion.12), channel_id=1, source_target_pairs={{0,1},{1,2},{2,3},{3,0},{4,5},{5,6},{6,7},{7,4},{8,9},{9,10},{10,1... | collective-permute-start | bytes 786440 | tf_op jit(solution)/shard_map/ppermute | solution.py:570
  47.0 41.5 %collective-permute-start.9 = (bf16[256,512]{1,0:T(8,128)(2,1)}, bf16[256,512]{1,0:T(8,128)(2,1)S(1)}, u32[]{:S(2)}, u32[]{:S(2)}) collective-permute-start(bf16[256,512]{1,0:T(8,128)(2,1)} %dynamic-slice_bitcast_fusion.12), channel_id=1, source_target_pairs={{0,2},{1,3},{2,0},{3,1},{4,6},{5,7},{6,4},{7,5},{8,10},{9,11},{10,... | collective-permute-start | bytes 786440 | tf_op jit(solution)/shard_map/ppermute | solution.py:570
  90.1 37.5 %collective-permute-start.18 = (bf16[512,256]{1,0:T(8,128)(2,1)S(1)}, bf16[512,256]{1,0:T(8,128)(2,1)S(1)}, u32[]{:S(2)}, u32[]{:S(2)}) collective-permute-start(bf16[512,256]{1,0:T(8,128)(2,1)S(1)} %get-tuple-element.213), channel_id=1, source_target_pairs={{0,0},{1,8},{2,4},{3,12},{4,1},{5,9},{6,5},{7,13},{8,2},{9,10},{10... | collective-permute-start | bytes 786440 | tf_op jit(solution)/shard_map/ppermute | solution.py:545
  94.1 39.6 %collective-permute-start.25 = (bf16[3,256,256]{2,1,0:T(8,128)(2,1)S(1)}, bf16[3,256,256]{2,1,0:T(8,128)(2,1)S(1)}, u32[]{:S(2)}, u32[]{:S(2)}) collective-permute-start(bf16[3,256,256]{2,1,0:T(8,128)(2,1)S(1)} %pad_maximum_fusion.5.r0), channel_id=1, source_target_pairs={{0,8},{8,0},{1,9},{9,1},{2,10},{10,2},{3,11},{11,3},{4,12},{12,4},... | collective-permute-start | bytes 1179656 | tf_op jit(solution)/shard_map/ppermute | solution.py:566
  105.2 65.2 %collective-permute-start.12 = (bf16[3,256,512]{2,1,0:T(8,128)(2,1)S(1)}, bf16[3,256,512]{2,1,0:T(8,128)(2,1)}, u32[]{:S(2)}, u32[]{:S(2)}) collective-permute-start(bf16[3,256,512]{2,1,0:T(8,128)(2,1)S(1)} %pad_maximum_fusion.1.r0), channel_id=1, source_target_pairs={{0,16},{16,0},{1,17},{17,1},{2,18},{18,2},{3,19},{19,3},{4,20},{20... | collective-permute-start | bytes 2359304 | tf_op jit(solution)/shard_map/ppermute | solution.py:566
  164.8 85.0 %collective-permute-start.28 = (bf16[512,1024]{1,0:T(8,128)(2,1)S(1)}, bf16[512,1024]{1,0:T(8,128)(2,1)S(1)}, u32[]{:S(2)}, u32[]{:S(2)}) collective-permute-start(bf16[512,1024]{1,0:T(8,128)(2,1)S(1)} %get-tuple-element.95.vo), channel_id=1, source_target_pairs={{0,8},{8,0},{1,9},{9,1},{2,10},{10,2},{3,11},{11,3},{4,12},{12,4},... | collective-permute-start | bytes 3145736 | tf_op jit(solution)/shard_map/ppermute | solution.py:566
  170.4 40.1 %collective-permute-start.11 = (bf16[3,256,512]{2,1,0:T(8,128)(2,1)S(1)}, bf16[3,256,512]{2,1,0:T(8,128)(2,1)S(1)}, u32[]{:S(2)}, u32[]{:S(2)}) collective-permute-start(bf16[3,256,512]{2,1,0:T(8,128)(2,1)S(1)} %pad_maximum_fusion.1.r0), channel_id=1, source_target_pairs={{0,8},{8,0},{1,9},{9,1},{2,10},{10,2},{3,11},{11,3},{4,12},{12,4},... | collective-permute-start | bytes 2359304 | tf_op jit(solution)/shard_map/ppermute | solution.py:566
  170.4 62.6 %collective-permute-start.13 = (bf16[3,256,512]{2,1,0:T(8,128)(2,1)}, bf16[3,256,512]{2,1,0:T(8,128)(2,1)S(1)}, u32[]{:S(2)}, u32[]{:S(2)}) collective-permute-start(bf16[3,256,512]{2,1,0:T(8,128)(2,1)} %collective-permute-done.12.r2), channel_id=1, source_target_pairs={{0,8},{8,0},{1,9},{9,1},{2,10},{10,2},{3,11},{11,3},{4,12},{12,4},... | collective-permute-start | bytes 2359304 | tf_op jit(solution)/shard_map/ppermute | solution.py:566
  179.2 61.0 %collective-permute-start.33 = (bf16[3,256,256]{2,1,0:T(8,128)(2,1)S(1)}, bf16[3,256,256]{2,1,0:T(8,128)(2,1)S(1)}, u32[]{:S(2)}, u32[]{:S(2)}) collective-permute-start(bf16[3,256,256]{2,1,0:T(8,128)(2,1)S(1)} %pad_maximum_fusion.6.r0), channel_id=1, source_target_pairs={{0,16},{16,0},{1,17},{17,1},{2,18},{18,2},{3,19},{19,3},{4,20},{20... | collective-permute-start | bytes 1179656 | tf_op jit(solution)/shard_map/ppermute | solution.py:566
  179.8 67.3 %collective-permute-start.34 = (bf16[3,256,256]{2,1,0:T(8,128)(2,1)}, bf16[3,256,256]{2,1,0:T(8,128)(2,1)S(1)}, u32[]{:S(2)}, u32[]{:S(2)}) collective-permute-start(bf16[3,256,256]{2,1,0:T(8,128)(2,1)} %collective-permute-done.32.r1), channel_id=1, source_target_pairs={{0,16},{16,0},{1,17},{17,1},{2,18},{18,2},{3,19},{19,3},{4,20},{20... | collective-permute-start | bytes 1179656 | tf_op jit(solution)/shard_map/ppermute | solution.py:566
  210.5 57.4 %collective-permute-start.36 = (f32[512,256]{1,0:T(8,128)S(1)}, f32[512,256]{1,0:T(8,128)}, u32[]{:S(2)}, u32[]{:S(2)}) collective-permute-start(f32[512,256]{1,0:T(8,128)S(1)} %get-tuple-element.190), channel_id=1, source_target_pairs={{0,0},{1,8},{2,4},{3,12},{4,1},{5,9},{6,5},{7,13},{8,2},{9,10},{10... | collective-permute-start | bytes 1572872 | tf_op jit(solution)/shard_map/ppermute | solution.py:545
  233.0 57.8 %collective-permute-start.37 = (f32[512,256]{1,0:T(8,128)S(1)}, f32[512,256]{1,0:T(8,128)}, u32[]{:S(2)}, u32[]{:S(2)}) collective-permute-start(f32[512,256]{1,0:T(8,128)S(1)} %get-tuple-element.191), channel_id=1, source_target_pairs={{0,8},{1,0},{2,12},{3,4},{4,9},{5,1},{6,13},{7,5},{8,10},{9,2},{10... | collective-permute-start | bytes 1572872 | tf_op jit(solution)/shard_map/ppermute | solution.py:545
  249.8 46.6 %collective-permute-start.40 = (f32[512,256]{1,0:T(8,128)}, f32[512,256]{1,0:T(8,128)}, u32[]{:S(2)}, u32[]{:S(2)}) collective-permute-start(f32[512,256]{1,0:T(8,128)} %get-tuple-element.189), channel_id=1, source_target_pairs={{0,0},{1,8},{2,4},{3,12},{4,1},{5,9},{6,5},{7,13},{8,2},{9,10},{10... | collective-permute-start | bytes 1572872 | tf_op jit(solution)/shard_map/ppermute | solution.py:545
  252.3 55.3 %collective-permute-start.41 = (f32[512,256]{1,0:T(8,128)}, f32[512,256]{1,0:T(8,128)}, u32[]{:S(2)}, u32[]{:S(2)}) collective-permute-start(f32[512,256]{1,0:T(8,128)} %get-tuple-element.188), channel_id=1, source_target_pairs={{0,8},{1,0},{2,12},{3,4},{4,9},{5,1},{6,13},{7,5},{8,10},{9,2},{10... | collective-permute-start | bytes 1572872 | tf_op jit(solution)/shard_map/ppermute | solution.py:545
  264.7 45.8 %collective-permute-start.35 = (bf16[512,512]{1,0:T(8,128)(2,1)}, bf16[512,512]{1,0:T(8,128)(2,1)S(1)}, u32[]{:S(2)}, u32[]{:S(2)}) collective-permute-start(bf16[512,512]{1,0:T(8,128)(2,1)} %get-tuple-element.98), channel_id=1, source_target_pairs={{0,4},{4,0},{1,5},{5,1},{2,6},{6,2},{3,7},{7,3},{8,12},{12,8},{9,1... | collective-permute-start | bytes 1572872 | tf_op jit(solution)/shard_map/ppermute | solution.py:566
  268.0 49.5 %collective-permute-start.52 = (bf16[3,512,256]{2,1,0:T(8,128)(2,1)}, bf16[3,512,256]{2,1,0:T(8,128)(2,1)}, u32[]{:S(2)}, u32[]{:S(2)}) collective-permute-start(bf16[3,512,256]{2,1,0:T(8,128)(2,1)} %pad_maximum_fusion.3.o0), channel_id=1, source_target_pairs={{0,8},{8,0},{1,9},{9,1},{2,10},{10,2},{3,11},{11,3},{4,12},{12,4},... | collective-permute-start | bytes 2359304 | tf_op jit(solution)/shard_map/ppermute | solution.py:566
  317.5 36.4 %collective-permute-start.54 = (bf16[3,512,256]{2,1,0:T(8,128)(2,1)}, bf16[3,512,256]{2,1,0:T(8,128)(2,1)S(1)}, u32[]{:S(2)}, u32[]{:S(2)}) collective-permute-start(bf16[3,512,256]{2,1,0:T(8,128)(2,1)} %collective-permute-done.52.o1), channel_id=1, source_target_pairs={{0,16},{16,0},{1,17},{17,1},{2,18},{18,2},{3,19},{19,3},{4,20},{20... | collective-permute-start | bytes 2359304 | tf_op jit(solution)/shard_map/ppermute | solution.py:566
  319.1 35.1 %collective-permute-start.48 = (bf16[3,256,512]{2,1,0:T(8,128)(2,1)}, bf16[3,256,512]{2,1,0:T(8,128)(2,1)S(1)}, u32[]{:S(2)}, u32[]{:S(2)}) collective-permute-start(bf16[3,256,512]{2,1,0:T(8,128)(2,1)} %collective-permute-done.47.i2), channel_id=1, source_target_pairs={{0,8},{8,0},{1,9},{9,1},{2,10},{10,2},{3,11},{11,3},{4,12},{12,4},... | collective-permute-start | bytes 2359304 | tf_op jit(solution)/shard_map/ppermute | solution.py:566
  394.7 72.0 %collective-permute-start.118 = (bf16[4,512,256]{2,1,0:T(8,128)(2,1)}, bf16[4,512,256]{2,1,0:T(8,128)(2,1)}, u32[]{:S(2)}, u32[]{:S(2)}) collective-permute-start(bf16[4,512,256]{2,1,0:T(8,128)(2,1)} %get-tuple-element.163), channel_id=1, source_target_pairs={{0,8},{8,0},{1,9},{9,1},{2,10},{10,2},{3,11},{11,3},{4,12},{12,4},... | collective-permute-start | bytes 3145736 | tf_op jit(solution)/shard_map/ppermute | solution.py:566
  403.2 69.3 %collective-permute-start.111 = (bf16[4,256,512]{2,1,0:T(8,128)(2,1)}, bf16[4,256,512]{2,1,0:T(8,128)(2,1)}, u32[]{:S(2)}, u32[]{:S(2)}) collective-permute-start(bf16[4,256,512]{2,1,0:T(8,128)(2,1)} %get-tuple-element.158), channel_id=1, source_target_pairs={{0,16},{16,0},{1,17},{17,1},{2,18},{18,2},{3,19},{19,3},{4,20},{20... | collective-permute-start | bytes 3145736 | tf_op jit(solution)/shard_map/ppermute | solution.py:566
  454.3 43.6 %collective-permute-start.117 = (bf16[4,512,256]{2,1,0:T(8,128)(2,1)S(1)}, bf16[4,512,256]{2,1,0:T(8,128)(2,1)}, u32[]{:S(2)}, u32[]{:S(2)}) collective-permute-start(bf16[4,512,256]{2,1,0:T(8,128)(2,1)S(1)} %copy-done.119), channel_id=1, source_target_pairs={{0,8},{8,0},{1,9},{9,1},{2,10},{10,2},{3,11},{11,3},{4,12},{12,4},... | collective-permute-start | bytes 3145736 | tf_op jit(solution)/shard_map/ppermute | solution.py:566
  482.9 38.1 %collective-permute-start.110 = (bf16[4,256,512]{2,1,0:T(8,128)(2,1)S(1)}, bf16[4,256,512]{2,1,0:T(8,128)(2,1)S(1)}, u32[]{:S(2)}, u32[]{:S(2)}) collective-permute-start(bf16[4,256,512]{2,1,0:T(8,128)(2,1)S(1)} %copy-done.117), channel_id=1, source_target_pairs={{0,16},{16,0},{1,17},{17,1},{2,18},{18,2},{3,19},{19,3},{4,20},{20... | collective-permute-start | bytes 3145736 | tf_op jit(solution)/shard_map/ppermute | solution.py:566
  495.6 70.9 %collective-permute-start.103 = (bf16[4,256,256]{2,1,0:T(8,128)(2,1)S(1)}, bf16[4,256,256]{2,1,0:T(8,128)(2,1)S(1)}, u32[]{:S(2)}, u32[]{:S(2)}) collective-permute-start(bf16[4,256,256]{2,1,0:T(8,128)(2,1)S(1)} %get-tuple-element.150), channel_id=1, source_target_pairs={{0,8},{8,0},{1,9},{9,1},{2,10},{10,2},{3,11},{11,3},{4,12},{12,4},... | collective-permute-start | bytes 1572872 | tf_op jit(solution)/shard_map/ppermute | solution.py:566
  498.0 72.4 %collective-permute-start.63 = (bf16[512,1024]{1,0:T(8,128)(2,1)}, bf16[512,1024]{1,0:T(8,128)(2,1)S(1)}, u32[]{:S(2)}, u32[]{:S(2)}) collective-permute-start(bf16[512,1024]{1,0:T(8,128)(2,1)} %get-tuple-element.117), channel_id=1, source_target_pairs={{0,8},{8,0},{1,9},{9,1},{2,10},{10,2},{3,11},{11,3},{4,12},{12,4},... | collective-permute-start | bytes 3145736 | tf_op jit(solution)/shard_map/ppermute | solution.py:566
  498.7 70.6 %collective-permute-start.105 = (bf16[4,256,256]{2,1,0:T(8,128)(2,1)S(1)}, bf16[4,256,256]{2,1,0:T(8,128)(2,1)S(1)}, u32[]{:S(2)}, u32[]{:S(2)}) collective-permute-start(bf16[4,256,256]{2,1,0:T(8,128)(2,1)S(1)} %add_convert_fusion.10), channel_id=1, source_target_pairs={{0,16},{16,0},{1,17},{17,1},{2,18},{18,2},{3,19},{19,3},{4,20},{20... | collective-permute-start | bytes 1572872 | tf_op jit(solution)/shard_map/ppermute | solution.py:566
  550.9 76.4 %collective-permute-start.97 = (bf16[4,256,512]{2,1,0:T(8,128)(2,1)}, bf16[4,256,512]{2,1,0:T(8,128)(2,1)}, u32[]{:S(2)}, u32[]{:S(2)}) collective-permute-start(bf16[4,256,512]{2,1,0:T(8,128)(2,1)} %get-tuple-element.146), channel_id=1, source_target_pairs={{0,16},{16,0},{1,17},{17,1},{2,18},{18,2},{3,19},{19,3},{4,20},{20... | collective-permute-start | bytes 3145736 | tf_op jit(solution)/shard_map/ppermute | solution.py:566
  551.8 33.1 %collective-permute-start.120 = (bf16[512,256]{1,0:T(8,128)(2,1)}, bf16[512,256]{1,0:T(8,128)(2,1)}, u32[]{:S(2)}, u32[]{:S(2)}) collective-permute-start(bf16[512,256]{1,0:T(8,128)(2,1)} %get-tuple-element.175), channel_id=1, source_target_pairs={{0,3},{1,0},{2,1},{3,2},{4,7},{5,4},{6,5},{7,6},{8,11},{9,8},{10,9... | collective-permute-start | bytes 786440 | tf_op jit(solution)/shard_map/ppermute | solution.py:570
  570.4 34.3 %collective-permute-start.113 = (bf16[256,512]{1,0:T(8,128)(2,1)}, bf16[256,512]{1,0:T(8,128)(2,1)}, u32[]{:S(2)}, u32[]{:S(2)}) collective-permute-start(bf16[256,512]{1,0:T(8,128)(2,1)} %get-tuple-element.178), channel_id=1, source_target_pairs={{0,3},{1,0},{2,1},{3,2},{4,7},{5,4},{6,5},{7,6},{8,11},{9,8},{10,9... | collective-permute-start | bytes 786440 | tf_op jit(solution)/shard_map/ppermute | solution.py:570
  629.0 74.1 %collective-permute-start.60 = (f32[512,256]{1,0:T(8,128)S(1)}, f32[512,256]{1,0:T(8,128)S(1)}, u32[]{:S(2)}, u32[]{:S(2)}) collective-permute-start(f32[512,256]{1,0:T(8,128)S(1)} %copy-done.137), channel_id=1, source_target_pairs={{0,0},{8,1},{4,2},{12,3},{1,4},{9,5},{5,6},{13,7},{2,8},{10,9},{6,... | collective-permute-start | bytes 1572872 | tf_op jit(solution)/shard_map/ppermute | solution.py:555
  633.4 71.4 %collective-permute-start.61 = (f32[512,256]{1,0:T(8,128)S(1)}, f32[512,256]{1,0:T(8,128)S(1)}, u32[]{:S(2)}, u32[]{:S(2)}) collective-permute-start(f32[512,256]{1,0:T(8,128)S(1)} %copy-done.136), channel_id=1, source_target_pairs={{8,0},{0,1},{12,2},{4,3},{9,4},{1,5},{13,6},{5,7},{10,8},{2,9},{14... | collective-permute-start | bytes 1572872 | tf_op jit(solution)/shard_map/ppermute | solution.py:555
  675.8 45.5 %collective-permute-start.96 = (bf16[4,256,512]{2,1,0:T(8,128)(2,1)S(1)}, bf16[4,256,512]{2,1,0:T(8,128)(2,1)S(1)}, u32[]{:S(2)}, u32[]{:S(2)}) collective-permute-start(bf16[4,256,512]{2,1,0:T(8,128)(2,1)S(1)} %copy-done.115), channel_id=1, source_target_pairs={{0,16},{16,0},{1,17},{17,1},{2,18},{18,2},{3,19},{19,3},{4,20},{20... | collective-permute-start | bytes 3145736 | tf_op jit(solution)/shard_map/ppermute | solution.py:566
  677.7 43.6 %collective-permute-start.98 = (bf16[4,256,512]{2,1,0:T(8,128)(2,1)S(1)}, bf16[4,256,512]{2,1,0:T(8,128)(2,1)S(1)}, u32[]{:S(2)}, u32[]{:S(2)}) collective-permute-start(bf16[4,256,512]{2,1,0:T(8,128)(2,1)S(1)} %add_convert_fusion.7), channel_id=1, source_target_pairs={{0,8},{8,0},{1,9},{9,1},{2,10},{10,2},{3,11},{11,3},{4,12},{12,4},... | collective-permute-start | bytes 3145736 | tf_op jit(solution)/shard_map/ppermute | solution.py:566
  (256 other events, 4728.7 us)

commit v2 on v1

--- a/solution.py
+++ b/solution.py
@@ -136,7 +136,8 @@
             return s
         lax.fori_loop(0, L, two, tuple(s0), unroll=4)
         m_ref[:, lanes] = ms[...]
-        low_ref[:, lanes] = silu(ms[...]).astype(bf16)
+        low_ref[:, lanes] = xs[...].astype(bf16)
+        low_ref[:, W + lt*LT : W + (lt+1)*LT] = silu(ms[...]).astype(bf16)
 
 def bwd_kernel(g_ref, m_ref, x_ref, par_ref, skip_ref, s0_ref, eg_ref, gp_ref, gm_ref, st_ref, xs, gs_ref, es):
     T, W = x_ref.shape
@@ -201,7 +202,7 @@
 
 def ema_fwd(x, par, skip):
     T,W = x.shape
-    return pl.pallas_call(fwd_kernel, out_shape=(jax.ShapeDtypeStruct((T,W),f32), jax.ShapeDtypeStruct((T,W),bf16), jax.ShapeDtypeStruct((HD,CH,W),f32)),
+    return pl.pallas_call(fwd_kernel, out_shape=(jax.ShapeDtypeStruct((T,W),f32), jax.ShapeDtypeStruct((T,2*W),bf16), jax.ShapeDtypeStruct((HD,CH,W),f32)),
         in_specs=[VM]*3, out_specs=(VM,VM,VM), name="ema_fwd", scratch_shapes=[pltpu.VMEM((T,LT),f32)]*2,
         compiler_params=pltpu.CompilerParams(vmem_limit_bytes=48<<20))(x,par,skip)
 def ema_bwd(g,m,x,par,skip,s0):
@@ -212,21 +213,26 @@
         compiler_params=pltpu.CompilerParams(vmem_limit_bytes=48<<20))(g,m,x,par,skip,s0)
 
 
-def tile(loc, rem, q, rel, s):
-    return loc[q ^ rel] if s == 0 else rem[rel][s - 1]
-
-
-def value_kernel(idx, n0, n1, o0, o1, loc, r0, r1, r2, r3, full, pre, val):
+def tile(loc, rem, q, rel, s, pick=None):
+    if s == 0:
+        return loc[q ^ rel]
+    return rem[rel][s - 1] if pick is None else rem[rel][s - 1, pick]
+
+
+def value_kernel(idx, n0, n1, o0, o1, gain, st, loc, r0, r1, r2, r3, full, pre, val, xs):
     z, q, c, x = idx[0], idx[1], idx[2], idx[3]
     rem = (r0, r1, r2, r3)
-    full[:, at(2 * c + x, 256)] = n0[...]
-    full[:, at(2 * c + 1 - x, 256)] = n1[...]
-    full[:, at(2 - 2 * c + x, 256)] = o0[...]
-    full[:, at(3 - 2 * c - x, 256)] = o1[...]
+    full[:, at(2 * c + x, 256)] = n0[:, 0:256]
+    full[:, at(2 * c + 1 - x, 256)] = n1[:, 0:256]
+    full[:, at(2 - 2 * c + x, 256)] = o0[:, 0:256]
+    full[:, at(3 - 2 * c - x, 256)] = o1[:, 0:256]
+    for j, v in enumerate((n0, n1)):
+        b = x if j == 0 else 1 - x
+        xs[:, at(b, 256)] = v[:, 0:256].astype(f32) / gain[:, at(2 * c + b, 256)] * st[:, 1:2] + st[:, 0:1]
     for s in range(4):
         acc = None
         for rel in range(4):
-            t = dot(full[:, at(q ^ rel, 256)], tile(loc, rem, q, rel, s))
+            t = dot(full[:, at(q ^ rel, 256)], tile(loc, rem, q, rel, s, 0))
             acc = t if acc is None else acc + t
         v = at(lax.rem(z + 4 - s, 4), 256)
         pre[:, v] = acc
@@ -234,19 +240,19 @@
 
 
 def proj_kernel(
-    idx, n0, n1, o0, o1, loc, r0, r1, r2, r3, wsl, ws1, ws2, ws3, aff,
+    idx, n0, n1, o0, o1, loc, r0, r1, r2, r3, ws, aff,
     full, reset, update, hidden, shp, qs, ks,
 ):
     z, q, c, x = idx[0], idx[1], idx[2], idx[3]
     rem = (r0, r1, r2, r3)
-    full[:, at(2 * c + x, 256)] = n0[...]
-    full[:, at(2 * c + 1 - x, 256)] = n1[...]
-    full[:, at(2 - 2 * c + x, 256)] = o0[...]
-    full[:, at(3 - 2 * c - x, 256)] = o1[...]
+    full[:, at(2 * c + x, 256)] = n0[:, 256:512]
+    full[:, at(2 * c + 1 - x, 256)] = n1[:, 256:512]
+    full[:, at(2 - 2 * c + x, 256)] = o0[:, 256:512]
+    full[:, at(3 - 2 * c - x, 256)] = o1[:, 256:512]
     rows = [full[:, at(lax.rem(z + 4 - s, 4), 256)] for s in range(4)]
     acc = None
-    for s, w in enumerate((wsl, ws1, ws2, ws3)):
-        t = dot(rows[s], w[...])
+    for s in range(4):
+        t = dot(rows[s], ws[lax.rem(z + 4 - s, 4)])
         acc = t if acc is None else acc + t
     shp[...] = acc
     sh = silu(acc)
@@ -299,7 +305,7 @@
     for rel in range(4):
         acc = None
         for s in range(4):
-            v = dot(gated[:, at(lax.rem(z + 4 - s, 4), 256)], tile(loc, rem, q, rel, s))
+            v = dot(gated[:, at(lax.rem(z + 4 - s, 4), 256)], tile(loc, rem, q, rel, s, 1))
             acc = v if acc is None else acc + v
         part[:, at(q ^ rel, 256)] = acc
     own[...] = part[:, at(c, 512)]
@@ -338,70 +344,64 @@
     full[:, at(1 - c, w)] = b[...]
 
 
+def quad(loc, rem, y, rel, s):
+    return loc[y ^ rel] if s == 0 else rem[rel][s - 1]
+
+
 def ffn_kernel(
-    idx, s0, s1, g0, g1, il, i0, i1, i2, i3, ol, o0, o1, o2, o3,
-    sf, gf, low, gffn, own, send, part,
+    idx, s0, s1, s2, s3, g0, g1, g2, g3, il, i0, i1, ol, o0, o1, sf, gf, low, gffn, top, bot, send, part,
 ):
-    q, c = idx[1], idx[2]
-    ri, ro = (i0, i1, i2, i3), (o0, o1, o2, o3)
-    join(sf, s0, s1, c)
-    join(gf, g0, g1, c)
+    y, c = idx[1] >> 1, idx[2]
+    t = s0.shape[0]
+    for full, blocks in ((sf, (s0, s1, s2, s3)), (gf, (g0, g1, g2, g3))):
+        for n, v in enumerate(blocks):
+            full[n // 2 * t : (n // 2 + 1) * t, at(1 - c if n % 2 else c, 512)] = v[...]
     for s in range(4):
-        f = slice(s * 512, (s + 1) * 512)
-        pre = None
-        for rel in range(4):
-            t = dot(sf[:, at(q ^ rel, 256)], tile(il, ri, q, rel, s))
-            pre = t if pre is None else pre + t
+        f = slice(s * 256, (s + 1) * 256)
+        pre = dot(sf[:, at(y, 512)], quad(il, (i0, i1), y, 0, s))
+        pre = pre + dot(sf[:, at(1 - y, 512)], quad(il, (i0, i1), y, 1, s))
         low[:, f] = silu(pre).astype(bf16)
-        g = None
-        for rel in range(4):
-            t = dot_t(gf[:, at(q ^ rel, 256)], tile(ol, ro, q, rel, s))
-            g = t if g is None else g + t
+        g = dot_t(gf[:, at(y, 512)], quad(ol, (o0, o1), y, 0, s))
+        g = g + dot_t(gf[:, at(1 - y, 512)], quad(ol, (o0, o1), y, 1, s))
         gffn[:, f] = (g * silu_grad(pre)).astype(bf16)
-    for rel in range(4):
+    for rel in range(2):
         acc = None
         for s in range(4):
-            t = dot_t(gffn[:, s * 512 : (s + 1) * 512], tile(il, ri, q, rel, s))
-            acc = t if acc is None else acc + t
-        part[:, at(q ^ rel, 256)] = acc
-    own[...] = part[:, at(c, 512)]
-    send[...] = part[:, at(1 - c, 512)].astype(bf16)
-
-
-def branch_kernel(idx, low, ol, o0, o1, o2, o3, own, send, part):
-    q, c = idx[1], idx[2]
-    ro = (o0, o1, o2, o3)
-    for rel in range(4):
+            v = dot_t(gffn[:, s * 256 : (s + 1) * 256], quad(il, (i0, i1), y, rel, s))
+            acc = v if acc is None else acc + v
+        part[y ^ rel] = acc
+    top[...] = part[c, 0:t]
+    bot[...] = part[c, t : 2 * t]
+    send[...] = part[1 - c].astype(bf16)
+
+
+def branch_kernel(idx, low, ol, o0, o1, top, bot, send, part):
+    y, c = idx[1] >> 1, idx[2]
+    t = top.shape[0]
+    for rel in range(2):
         acc = None
         for s in range(4):
-            t = dot(low[:, s * 512 : (s + 1) * 512], tile(ol, ro, q, rel, s))
-            acc = t if acc is None else acc + t
-        part[:, at(q ^ rel, 256)] = acc
-    own[...] = part[:, at(c, 512)]
-    send[...] = part[:, at(1 - c, 512)].astype(bf16)
-
-
-def grad_out_kernel(idx, low, gf, *outs):
-    q = idx[1]
-    n = outs[0].shape[1]
-    for s in range(4):
-        a = low[:, s * n : (s + 1) * n]
-        for rel in range(4):
-            outs[rel][s] = t_dot(a, gf[:, at(q ^ rel, 256)]).astype(bf16)
-
-
-def grad_in_kernel(idx, sf, gffn, *outs):
-    q = idx[1]
-    n = outs[0].shape[2]
-    for rel in range(4):
-        a = sf[:, at(q ^ rel, 256)]
+            v = dot(low[:, s * 256 : (s + 1) * 256], quad(ol, (o0, o1), y, rel, s))
+            acc = v if acc is None else acc + v
+        part[y ^ rel] = acc
+    top[...] = part[c, 0:t]
+    bot[...] = part[c, t : 2 * t]
+    send[...] = part[1 - c].astype(bf16)
+
+
+def grad_ffn_kernel(idx, low, gf, sf, gffn, keep, send):
+    z, y = idx[0], idx[1] >> 1
+    for n, (a, b) in enumerate(((low, gf), (gffn, sf))):
         for s in range(4):
-            outs[rel][s] = t_dot(a, gffn[:, s * n : (s + 1) * n]).astype(bf16)
-
-
-def grad_unit_kernel(idx, own, recv, state, st, so, gain, gu, st2, gno):
+            v = a[:, s * 256 : (s + 1) * 256]
+            p = lax.rem(z + 4 - s, 4)
+            keep[p, n] = t_dot(v, b[:, at(y, 512)]).astype(bf16)
+            send[p, n] = t_dot(v, b[:, at(1 - y, 512)]).astype(bf16)
+
+
+def grad_unit_kernel(idx, own, recv, xrecv, state, st, so, gain, gu, st2, gno):
     unit, _ = unit_of(state, st, so)
-    g = own[...] + recv[...].astype(f32)
+    g = own[...] + recv[0 : own.shape[0], :].astype(f32) + xrecv[...].astype(f32)
     gu[...] = g
     gno[...] = jnp.sum(g * unit, axis=0, keepdims=True)
     gn = g * gain[...]
@@ -422,7 +422,7 @@
     s = sig(h)
     ug[...] = (gs * (h * s - xs[...]) * u * (1.0 - u)).astype(bf16)
     hg[...] = (gs * u * (s * (1.0 + h * (1.0 - s)))).astype(bf16)
-    gi[...] = gs * (1.0 - u)
+    gi[...] = (gs * (1.0 - u)).astype(bf16)
 
 
 def gate_kernel(
@@ -436,7 +436,7 @@
         v = at(lax.rem(z + 4 - s, 4), 256)
         g = None
         for rel in range(4):
-            w = dot_t(hf[:, at(q ^ rel, 256)], tile(loc, rem, q, rel, s))
+            w = dot_t(hf[:, at(q ^ rel, 256)], tile(loc, rem, q, rel, s, 1))
             g = w if g is None else g + w
         r = reset[:, v]
         sg = sig(r)
@@ -463,65 +463,63 @@
     vown[...] = t_dot(probs[:, 0:t], gatt[...])
 
 
-def value_back_kernel(idx, vown, vrecv, pre, loc, r0, r1, r2, r3, gv, own, send, part):
+def mixer_back_kernel(
+    idx, vown, recv, pre, vloc, v0, v1, v2, v3, cat, loc, r0, r1, r2, r3, ws, aff, shp, qg, kown,
+    gv, gs, ga, own, send, part,
+):
     z, q, c = idx[0], idx[1], idx[2]
     rem = (r0, r1, r2, r3)
-    gv[...] = ((vown[...] + vrecv[...].astype(f32)) * silu_grad(pre[...])).astype(bf16)
+    d = vown.shape[1]
+    gv[...] = ((vown[...] + recv[:, 0:d].astype(f32)) * silu_grad(pre[...])).astype(bf16)
     for rel in range(4):
         acc = None
         for s in range(4):
-            w = dot_t(gv[:, at(lax.rem(z + 4 - s, 4), 256)], tile(loc, rem, q, rel, s))
+            w = dot_t(gv[:, at(lax.rem(z + 4 - s, 4), 256)], tile(vloc, (v0, v1, v2, v3), q, rel, s, 0))
             acc = w if acc is None else acc + w
         part[:, at(q ^ rel, 256)] = acc
-    own[...] = part[:, at(c, 512)]
-    send[...] = part[:, at(1 - c, 512)].astype(bf16)
-
-
-def mixer_back_kernel(
-    idx, cat, loc, r0, r1, r2, r3, wsl, ws1, ws2, ws3, aff, shp, qg, kown, krecv, gs, ga, own, send, part,
-):
-    z, q, c = idx[0], idx[1], idx[2]
-    rem = (r0, r1, r2, r3)
-    kg = kown[...] + krecv[...].astype(f32)
+    own[1] = part[:, at(c, 512)]
+    send[1] = part[:, at(1 - c, 512)].astype(bf16)
+    kg = kown[...] + recv[:, d:].astype(f32)
     s_pre = shp[...]
     sh = silu(s_pre)
     g = qg[...]
     gs[...] = ((g * aff[0:1, :] + kg * aff[2:3, :]) * silu_grad(s_pre)).astype(bf16)
-    ga[0:1, :] = jnp.sum(g * sh, axis=0, keepdims=True)
-    ga[1:2, :] = jnp.sum(g, axis=0, keepdims=True)
-    ga[2:3, :] = jnp.sum(kg * sh, axis=0, keepdims=True)
-    for s, w in enumerate((wsl, ws1, ws2, ws3)):
-        acc = dot_t(gs[...], w[...])
+    rows = [jnp.sum(v, axis=0, keepdims=True) for v in (g * sh, g, kg * sh)]
+    ga[...] = jnp.concatenate(rows + [jnp.zeros((5, g.shape[1]), f32)], 0)
+    for s in range(4):
+        acc = dot_t(gs[...], ws[lax.rem(z + 4 - s, 4)])
         for rel in range(4):
             acc = acc + dot_t(cat[rel], tile(loc, rem, q, rel, s))
         part[:, at(lax.rem(z + 4 - s, 4), 256)] = acc
-    own[...] = part[:, at(c, 512)]
-    send[...] = part[:, at(1 - c, 512)].astype(bf16)
-
-
-def grad_pack_kernel(idx, mf, cat, *outs):
+    own[0] = part[:, at(c, 512)]
+    send[0] = part[:, at(1 - c, 512)].astype(bf16)
+
+
+def grad_pack_kernel(idx, mf, cat, keep, send):
     z = idx[0]
     for s in range(4):
         a = mf[:, at(lax.rem(z + 4 - s, 4), 256)]
         for rel in range(4):
-            outs[rel][s] = t_dot(a, cat[rel]).astype(bf16)
-
-
-def grad_u_kernel(idx, gated, hf, *outs):
+            out = send if rel & 2 else keep
+            out[rel & 1, lax.rem(z + 4 - s, 4)] = t_dot(a, cat[rel]).astype(bf16)
+
+
+def grad_u_kernel(idx, gated, hf, keep, send):
     z, q = idx[0], idx[1]
     for s in range(4):
         a = gated[:, at(lax.rem(z + 4 - s, 4), 256)]
         for rel in range(4):
-            outs[rel][s] = t_dot(a, hf[:, at(q ^ rel, 256)]).astype(bf16)
-
-
-def grad_value_kernel(idx, nf, gv, mf, gs, o0, o1, o2, o3, gws):
+            out = send if rel & 1 else keep
+            out[rel >> 1, lax.rem(z + 4 - s, 4)] = t_dot(a, hf[:, at(q ^ rel, 256)]).astype(bf16)
+
+
+def grad_value_kernel(idx, nf, gv, mf, gs, keep, send, gws):
     z, q = idx[0], idx[1]
-    outs = (o0, o1, o2, o3)
     for rel in range(4):
         a = nf[:, at(q ^ rel, 256)]
         for s in range(4):
-            outs[rel][s] = t_dot(a, gv[:, at(lax.rem(z + 4 - s, 4), 256)]).astype(bf16)
+            out = send if rel & 1 else keep
+            out[rel >> 1, lax.rem(z + 4 - s, 4)] = t_dot(a, gv[:, at(lax.rem(z + 4 - s, 4), 256)]).astype(bf16)
     gws[...] = t_dot(mf[...], gs[...])
 
 
@@ -562,6 +560,10 @@
     return pick(z % 2 == 0, r[0], r[1], 0)
 
 
+def after(v, *deps):
+    return lax.optimization_barrier((v,) + deps)[0]
+
+
 def swap2(a, axis):
     return lax.ppermute(a, axis, [(0, 1), (1, 0)])
 
@@ -591,12 +593,16 @@
     return lax.psum(v, "rest") if rest > 1 else v
 
 
-def gather(loc, q, x_first):
-    mine = lax.dynamic_index_in_dim(loc, q, 0, False)
-    three = jnp.stack([shifted(mine, "tensor", 4, s) for s in range(1, 4)])
+def others(every, z):
+    return jnp.concatenate(
+        [lax.dynamic_slice_in_dim(every, (z + 4 - s) % 4, 1, 0) for s in range(1, 4)]
+    )
+
+
+def spread_plane(three, *deps):
     nx = swap2(three, "xx")
     ny = swap2(three, "yy")
-    nxy = swap2(nx, "yy") if x_first else swap2(ny, "xx")
+    nxy = swap2(after(nx, *deps), "yy")
     return [three, nx, ny, nxy]
 
 
@@ -604,16 +610,24 @@
     return (a.astype(f32) + b.astype(f32)).astype(bf16)
 
 
-def reduce_blocks(g, rest, x_first):
+def reduce_plane(keep, send, first, second, dep):
+    pair = add(keep, after(swap2(send, first), dep))
+    return add(pair[0], swap2(pair[1], second))
+
+
+def reduce_tensor(own, rest):
     if rest > 1:
-        g = [lax.psum(v, "rest") for v in g]
-    first, second, near, far = ("xx", "yy", 1, 2) if x_first else ("yy", "xx", 2, 1)
-    own = add(g[0], swap2(g[near], first))
-    side = add(g[far], swap2(g[3], first))
-    own = add(own, swap2(side, second))
-    total = own[0].astype(f32)
+        own = lax.psum(own, "rest")
+    return lax.psum_scatter(own, "tensor", scatter_dimension=0)
+
+
+def reduce_tensor_direct(own, rest, z):
+    if rest > 1:
+        own = lax.psum(own, "rest")
+    total = lax.dynamic_index_in_dim(own, z, 0, False).astype(f32)
     for s in range(1, 4):
-        total = total + shifted(own[s], "tensor", 4, 4 - s).astype(f32)
+        v = lax.dynamic_index_in_dim(own, (z + s) % 4, 0, False)
+        total = total + shifted(v, "tensor", 4, s).astype(f32)
     return total
 
 
@@ -659,19 +673,7 @@
         n = a.shape[1] // 4
         return jnp.stack([a[:, i * n : (i + 1) * n] for i in range(4)])
 
-    starts = lax.ppermute(piece_starts, GROUP, place(0))[0]
-    idx = jnp.concatenate([jnp.stack([z, q, c, x]).astype(jnp.int32), starts])
-
-    norm_in_own = lax.dynamic_slice_in_dim(norm_in, z * width, width, 0)
-    mean_in, inv_in = moments(inputs, "tensor", 4)
-    unit_in = (inputs - mean_in) * inv_in
-    normed = unit_in * norm_in_own
-    par = jnp.concatenate([expand.T, ema_rate.T, damping.T, project.T], 0)
-    skip = ema_skip[None, :]
-    nb = to_chips(normed.astype(bf16))
-    mixed, mixer_low, s0 = ema_fwd(normed, par, skip)
-    mb = to_chips(mixer_low)
-
+    y = q // 2
     lv = by_rows(half(w_value, 1))
     k = w_reset.shape[0]
     vq = w_reset.shape[1] // 4
@@ -680,46 +682,82 @@
         [jnp.moveaxis(wr4, 1, 0), by_cols(half(w_update, 1)), by_cols(half(w_hidden, 1))], 2
     )
     lu = by_cols(half(u_hidden, 0))
-    li = by_rows(half(w_in, 1))
-    lo = by_cols(half(w_out, 0))
-    wv = [lv] + gather(lv, q, True)
-    wsh = [w_shared] + [shifted(w_shared, "tensor", 4, s) for s in range(1, 4)]
-    wp = [lp] + gather(lp, q, False)
-    wu = [lu] + gather(lu, q, True)
-    wi = [li] + gather(li, q, False)
-    wo = [lo] + gather(lo, q, True)
-
-    x_sp = to_chips(inputs)
-    x_sp = pick(x == 0, x_sp[0], x_sp[1], 1)
-    cot = to_chips(cotangent)
-    cot = pick(x == 0, cot[0], cot[1], 1)
-    cot_low = cot.astype(bf16)
-    cot_other = swap2(cot_low, "core")
-
-    nf, value_pre, values = call(
+    fq = w_in.shape[1] // 4
+    li = lax.dynamic_slice_in_dim(w_in, (c * 2 + x) * fq, fq, 1).reshape(2, d // 2, fq)
+    lo = lax.dynamic_slice_in_dim(w_out, (c * 2 + x) * fq, fq, 0)
+    lo = jnp.stack([lo[:, : d // 2], lo[:, d // 2 :]])
+
+    def part(a, i):
+        return lax.dynamic_index_in_dim(a, i, 0, False)
+
+    def planes(a):
+        return lax.all_gather(a, "tensor", axis=0)
+
+    nq, nc = d // 4, w_value.shape[1] // 2
+    first = jnp.stack(
+        [
+            lax.dynamic_slice(w_value, (q * nq, c * nc), (nq, nc)),
+            lax.dynamic_slice(u_hidden, (c * nc, q * nq), (nc, nq)),
+        ]
+    )
+    norm_in_own = lax.dynamic_slice_in_dim(norm_in, z * width, width, 0)
+    mean_in, inv_in = moments(after(inputs, first), "tensor", 4)
+    starts = piece_starts[0].astype(f32)
+    about = jnp.stack([mean_in[:, 0], 1.0 / inv_in[:, 0]])
+    about = lax.dynamic_slice_in_dim(about, (z % 2) * t, t, 1)
+    about = jnp.concatenate([about, jnp.pad(starts, (0, t - 2))[None]])
+    unit_in = (inputs - mean_in) * inv_in
+    normed = unit_in * norm_in_own
+    par = jnp.concatenate([expand.T, ema_rate.T, damping.T, project.T], 0)
+    skip = ema_skip[None, :]
+    mixed, both_low, s0 = ema_fwd(normed, par, skip)
+    nm = to_chips(both_low)
+    about = lax.ppermute(about, GROUP, place(0))
+    starts = about[2, 0:2].astype(jnp.int32)
+    idx = jnp.concatenate([jnp.stack([z, q, c, x]).astype(jnp.int32), starts])
+    about = about[0:2].T
+
+    ac = others(planes(first), z)
+    ac = spread_plane(after(ac, both_low), *nm)
+    nm = nm + [swap2(after(b, ac[1], ac[2]), "core") for b in nm]
+    pk = planes(after(jnp.concatenate([part(lp, q), w_shared], 1), *nm[:2]))
+    wv, wu = [lv] + ac, [lu] + ac
+
+    nf, value_pre, values, x_sp = call(
         value_kernel,
-        [shape((t, d), bf16), shape((t, d), f32), shape((t, d), bf16)],
-        idx, *nb, *[swap2(b, "core") for b in nb], *wv, name="value",
+        [shape((t, d), bf16), shape((t, d), f32), shape((t, d), bf16), shape((t, dh), f32)],
+        idx, *nm, norm_in[None, :], about, *wv, name="value",
     )
     values_n = swap2(values, "xx")
+    ws = after(pk, values)[:, :, lp.shape[2] :]
+    wp = [lp] + spread_plane(others(after(pk[:, :, : lp.shape[2]], values), z))
+    cot = to_chips(after(cotangent.astype(bf16), *nm[:2]))
+    cot_low = pick(x == 0, cot[0], cot[1], 1)
+    cot_core = swap2(cot_low, "core")
+    cot_x = swap2(after(cot_low, wp[3]), "xx")
+    cots = [cot_low, cot_core, cot_x, swap2(cot_x, "core")]
     mf, reset, update, hidden, shp, qs, ks = call(
         proj_kernel,
         [
             shape((t, d), bf16), shape((t, d), f32), shape((t, dh), f32), shape((t, dh), f32),
             shape((t, 128), f32), shape((t, 128), bf16), shape((t, 128), bf16),
         ],
-        idx, *mb, *[swap2(b, "core") for b in mb], *wp, *wsh, qk_affine, name="proj",
+        idx, *nm, *wp, ws, after(qk_affine, cot_low), name="proj",
     )
     ks_n = swap2(ks, "xx")
+    wi = others(after(planes(part(li, y)), qs), z)
+    wi = [li, wi, swap2(wi, "yy")]
     probs, att, gated, own, send = call(
         attend_kernel,
         [
             shape((t, 2 * t), bf16), shape((t, d), f32), shape((t, d), bf16),
             shape((t, dh), f32), shape((t, dh), bf16),
         ],
-        idx, qs, ks, ks_n, values, values_n, reset, *wu, name="attend",
+        idx, qs, ks, ks_n, values, values_n, after(reset, *cots), *wu, name="attend",
         scratch=[pltpu.VMEM((t, d), f32)],
     )
+    wo = others(after(planes(part(lo, y)), gated), z)
+    wo = [lo, wo, swap2(wo, "yy")]
     gain = lax.dynamic_slice_in_dim(norm_out, c * dh, dh, 0)[None, :]
     half_f = shape((t, dh), f32)
     half_b = shape((t, dh), bf16)
@@ -730,110 +768,126 @@
     so = swap2(st, "core")
     (low,) = call(unit_kernel, [half_b], idx, state, st, so, gain, name="unit")
 
-    sf, gf, ffn_low, gffn, own, send = call(
+    def blocks(r, m):
+        return [shape((4, r, m), bf16)] * 4
+
+    low_x = swap2(low, "xx")
+    f_out = [half_f, half_f, shape((2 * t, dh), bf16)]
+    sf, gf, ffn_low, gffn, top, bot, send = call(
         ffn_kernel,
-        [shape((t, d), bf16), shape((t, d), bf16), shape((t, 2 * d), bf16), shape((t, 2 * d), bf16), half_f, half_b],
-        idx, low, swap2(low, "core"), cot_low, cot_other, *wi, *wo, name="ffn",
-        scratch=[pltpu.VMEM((t, d), f32)],
-    )
+        [shape((2 * t, d), bf16)] * 4 + f_out,
+        idx, low, swap2(low, "core"), low_x, swap2(low_x, "core"), *cots, *wi, *wo, name="ffn",
+        scratch=[pltpu.VMEM((2, 2 * t, dh), f32)],
+    )
+
+    def over_x(bot, recv):
+        return (bot + recv[t:].astype(f32)).astype(bf16)
+
+    recv = swap2(send, "core")
+    x_send = over_x(bot, recv)
+    b_top, b_bot, b_send = call(
+        branch_kernel, f_out, idx, after(ffn_low, x_send), *wo, name="branch", scratch=[pltpu.VMEM((2, 2 * t, dh), f32)]
+    )
+    f_keep, f_send = call(
+        grad_ffn_kernel, [shape((4, 2, 256, 512), bf16)] * 2, idx, ffn_low, gf, sf, after(gffn, x_send), name="grad_ffn"
+    )
+    f_recv = swap2(f_send, "yy")
     gunit, st2, gno = call(
         grad_unit_kernel, [half_f, stat, shape((1, dh), f32)],
-        idx, own, swap2(send, "core"), state, st, so, gain, name="grad_unit",
-    )
+        idx, after(top, b_top, f_keep), recv, swap2(x_send, "xx"), state, st, so, gain, name="grad_unit",
+    )
+    cot = cot_low
     ug, hg, gi = call(
-        grad_state_kernel, [half_b, half_b, half_f],
+        grad_state_kernel, [half_b, half_b, half_b],
         idx, gunit, state, st, so, st2, swap2(st2, "core"), gain, cot, hpre, update, x_sp, name="grad_state",
     )
-    gi_direct = from_chips(gi)
-    own, send = call(
-        branch_kernel, [half_f, half_b], idx, ffn_low, *wo, name="branch", scratch=[pltpu.VMEM((t, d), f32)]
-    )
-    outputs = from_chips(state + own + swap2(send, "core").astype(f32))
-
-    def blocks(r, m):
-        return [shape((4, r, m), bf16)] * 4
-
-    g_wo = call(grad_out_kernel, blocks(512, 256), idx, ffn_low, gf, name="grad_w_out")
-    g_wi = call(grad_in_kernel, blocks(256, 512), idx, sf, gffn, name="grad_w_in")
-    r_wo = reduce_blocks(g_wo, rest, True)
-    r_wi = reduce_blocks(g_wi, rest, False)
-
+
+    b_recv = swap2(b_send, "core")
+    b_x = over_x(b_bot, b_recv)
     hf, cat, gatt, vsend = call(
         gate_kernel,
         [shape((t, d), bf16), shape((4, t, 512), bf16), shape((t, d), bf16), shape((t, d), bf16)],
-        idx, hg, swap2(hg, "core"), ug, reset, att, probs, *wu, name="gate",
+        idx, hg, swap2(hg, "core"), after(ug, b_x), reset, att, probs, *wu, name="gate",
         scratch=[pltpu.VMEM((t, d), bf16)],
     )
-    vrecv = swap2(vsend, "xx")
     qg, kown, ksend, vown = call(
         attend_back_kernel,
         [shape((t, 128), f32), shape((t, 128), f32), shape((t, 128), bf16), shape((t, d), f32)],
         idx, probs, gatt, values, values_n, ks, ks_n, qs, name="attend_back",
     )
-    g_uh = call(grad_u_kernel, blocks(256, 256), idx, gated, hf, name="grad_u_hidden")
-    g_pk = call(grad_pack_kernel, blocks(256, 512), idx, mf, cat, name="grad_pack")
-    r_uh = reduce_blocks(g_uh, rest, True)
-    r_pk = reduce_blocks(g_pk, rest, False)
-    gs, ga, own, send = call(
+    out = (state + b_top + b_recv[:t].astype(f32) + swap2(b_x, "xx").astype(f32)).astype(bf16)
+    back = jnp.concatenate([out[:, :width], gi[:, :width], out[:, width:], gi[:, width:]], 1)
+    mf = after(mf, back)
+    back = from_chips(back)
+    kv_recv = swap2(jnp.concatenate([vsend, ksend], 1), "xx")
+    f_sum = add(f_keep, after(f_recv, qg))
+    r_ffn = reduce_tensor(f_sum, rest)
+    r_wo, r_wi = r_ffn[0], r_ffn[1]
+    two = [shape((2, 4, 256, 256), bf16)] * 2
+    g_uh = call(grad_u_kernel, two, idx, gated, hf, name="grad_u_hidden")
+    g_pk = call(grad_pack_kernel, [shape((2, 4, 256, 512), bf16)] * 2, idx, mf, cat, name="grad_pack")
+    gv, gs, ga, own, send = call(
         mixer_back_kernel,
-        [shape((t, 128), bf16), shape((3, 128), f32), half_f, half_b],
-        idx, cat, *wp, *wsh, qk_affine, shp, qg, kown, swap2(ksend, "xx"), name="mixer_back",
+        [shape((t, d), bf16), shape((t, 128), bf16), shape((8, 128), f32), shape((2, t, dh), f32), shape((2, t, dh), bf16)],
+        idx, vown, kv_recv, value_pre, *wv, after(cat, g_uh[0], g_pk[0], f_sum, back), *wp, ws, qk_affine, shp, qg, kown,
+        name="mixer_back", limit=56,
         scratch=[pltpu.VMEM((t, d), f32)],
     )
-    grad_mixer = from_chips((own + swap2(send, "core").astype(f32)).astype(bf16))
-    gv, own, send = call(
-        value_back_kernel, [shape((t, d), bf16), half_f, half_b],
-        idx, vown, vrecv, value_pre, *wv, name="value_back", scratch=[pltpu.VMEM((t, d), f32)],
-    )
-    normed_part = from_chips((own + swap2(send, "core").astype(f32)).astype(bf16))
-    *g_wv, g_ws = call(
-        grad_value_kernel, blocks(256, 256) + [shape((d, 128), f32)], idx, nf, gv, mf, gs, name="grad_w_value"
-    )
-    r_wv = reduce_blocks(g_wv, rest, True)
-
-    ema_grad, g_par = ema_bwd(grad_mixer, mixed, normed, par, skip, s0)
+    both = (own + swap2(send, "core").astype(f32)).astype(bf16)
+    both = jnp.concatenate([both[0, :, :width], both[1, :, :width], both[0, :, width:], both[1, :, width:]], 1)
+    both = from_chips(both)
+    grad_mixer, normed_part = both[:, :width], both[:, width:]
+    *g_wv, gws = call(grad_value_kernel, two + [shape((d, 128), f32)], idx, nf, gv, mf, gs, name="grad_w_value")
+    pair_pk = add(g_pk[0], swap2(g_pk[1], "yy"))
+    pair_uh = add(g_uh[0], swap2(g_uh[1], "xx"))
+    ema_grad, g_par = ema_bwd(after(grad_mixer, g_wv[0], pair_pk, pair_uh), mixed, normed, par, skip, s0)
+    outputs = back[:, :width].astype(f32)
+    gi_direct = back[:, width:].astype(f32)
+    p_pk = add(pair_pk[0], swap2(pair_pk[1], "xx"))
+    p_uh = add(pair_uh[0], swap2(pair_uh[1], "yy"))
+    p_wv = reduce_plane(*g_wv, "xx", "yy", ema_grad)
     grad_normed = normed_part.astype(f32) + ema_grad
     g_norm_in = jnp.sum(grad_normed * unit_in, axis=0)
     gn = grad_normed * norm_in_own
     sums = sum_over(jnp.stack([jnp.sum(gn, 1), jnp.sum(gn * unit_in, 1)]), "tensor", 4) / d
     grad_inputs = gi_direct + inv_in * (gn - sums[0][:, None] - unit_in * sums[1][:, None])
 
+    r_pk = reduce_tensor_direct(p_pk, rest, z)
+    r_all = reduce_tensor_direct(jnp.concatenate([p_uh, p_wv], 2), rest, z)
+    r_uh, r_wv = r_all[:, 0:256], r_all[:, 256:]
+
+    wide = lax.dynamic_update_slice(jnp.zeros((d,), f32), gno[0], (c * dh,)).reshape(4, 2, 128)
+    wide = jnp.concatenate([wide, jnp.stack([ga] * 4), jnp.zeros((4, 6, 128), f32), gws.reshape(4, width, 128)], 1)
+    wide = lax.psum_scatter(after(wide.astype(bf16), r_wo), "tensor", scatter_dimension=0).astype(f32)
     near = ("core", "xx", "yy")
-    small = sum_devices(jnp.concatenate([g_par, g_norm_in[None, :]], 0), rest, near)
-    wide = jnp.concatenate(
-        [lax.dynamic_update_slice(jnp.zeros((d,), f32), gno[0], (c * dh,)), ga.reshape(-1)]
-    )
-    wide = sum_devices(wide.reshape(-1, 128), rest, near + ("tensor",)).reshape(-1)
-    gno = lax.dynamic_slice_in_dim(wide, z * width, width, 0)
-    gaff = wide[d:].reshape(3, -1)
-
-    g_ws = g_ws.astype(bf16).reshape(4, width, 128)
-    part = lax.dynamic_index_in_dim(g_ws, z, 0, False).astype(f32)
-    for s in range(1, 4):
-        part = part + shifted(
-            lax.dynamic_index_in_dim(g_ws, (z + s) % 4, 0, False), "tensor", 4, s
-        ).astype(f32)
-    part = sum_devices(part, rest, near)
+    small = jnp.concatenate([g_par, g_norm_in[None, :]], 0)
+    small = sum_devices(jnp.concatenate([small[:, :128], small[:, 128:], wide], 0), rest, near)
+    wide = small[146:]
+    small = jnp.concatenate([small[:73], small[73:146]], 1)
+    gno, gaff = wide[0:2].reshape(-1), wide[2:5]
     dp = rest * 8
     me = lax.axis_index(DPS)
-    o_ws = lax.dynamic_slice_in_dim(part, me * (128 // dp), 128 // dp, 1)
+    o_ws = lax.dynamic_slice_in_dim(wide[16:], me * (128 // dp), 128 // dp, 1)
 
     r = lax.axis_index("rest")
 
-    def swap_join(g, dim, other):
+    def split_join(g, dim, axis):
+        i = lax.axis_index(axis)
+        n = g.shape[dim] // 2
+        keep = lax.dynamic_slice_in_dim(g, i * n, n, dim)
+        send = lax.dynamic_slice_in_dim(g, (1 - i) * n, n, dim)
+        return pick(i == 0, keep, swap2(send, axis), 1 - dim)
+
+    def finish(g, dim):
         if rest > 1:
             n = g.shape[dim] // rest
             g = lax.dynamic_slice_in_dim(g, r * n, n, dim)
-        n = g.shape[dim] // 2
-        keep = lax.dynamic_slice_in_dim(g, c * n, n, dim)
-        send = lax.dynamic_slice_in_dim(g, (1 - c) * n, n, dim)
-        return pick(c == 0, keep, swap2(send, "core"), other)
-
-    o_wv = swap_join(r_wv, 0, 1)
-    o_wi = swap_join(r_wi, 0, 1)
-    o_wo = swap_join(r_wo, 1, 0)
-    o_uh = swap_join(r_uh, 1, 0)
-    o_wr, both = r_pk[:, 0:256], r_pk[:, 256:512]
+        return split_join(g, dim, "core").astype(f32)
+    o_wv = finish(r_wv.astype(bf16), 0)
+    o_wi = finish(split_join(r_wi, 1, "xx"), 1).T
+    o_wo = finish(split_join(r_wo, 1, "xx"), 1)
+    o_uh = finish(r_uh.astype(bf16), 1)
+    o_wr, both = r_pk[:, 0:256], r_pk[:, 256:512].astype(bf16)
     if rest > 1:
         n = o_wr.shape[1] // rest
         o_wr = lax.all_gather(o_wr, "core", axis=1, tiled=True)
@@ -843,6 +897,7 @@
     else:
         both = lax.ppermute(both, PLANE + ("core",), [(b % 4 * 2 + b // 4, b) for b in range(8)])
         o_wu, o_wh = both[:, 0:128], both[:, 128:256]
+    o_wr, o_wu, o_wh = o_wr.astype(f32), o_wu.astype(f32), o_wh.astype(f32)
     return (
         outputs,
         grad_inputs,

time: 775 us -> 607 us (0.78)
  starting transfers between devices: 174 us -> 74.9 us
  waiting for transfers between devices: 379 us -> 296 us
  between operations: 2.87 us -> 16.1 us
  local copies, waits for them, and re-layouts: 65.8 us -> 55.7 us
    ppermute x45 -> x12, waiting for transfers between devices: 118 us -> 26.3 us  [shifted(): return lax.ppermute(a, axis, [(i, (i + s) % count) for i in range(count)])]
    ppermute x61 -> x44, waiting for transfers between devices: 183 us -> 108 us  [swap2(): return lax.ppermute(a, axis, [(0, 1), (1, 0)])]
    ppermute x8 -> x4, waiting for transfers between devices: 33.1 us -> 79.6 us  [to_chips(): lax.ppermute(lax.dynamic_index_in_dim(halves, (z + k) % 2, 0, False), GRO...]
    ppermute x45 -> x12, starting transfers between devices: 62.3 us -> 16.3 us  [shifted(): return lax.ppermute(a, axis, [(i, (i + s) % count) for i in range(count)])]
    ppermute x61 -> x44, starting transfers between devices: 71 us -> 34.4 us  [swap2(): return lax.ppermute(a, axis, [(0, 1), (1, 0)])]
    ppermute x8 -> x4, waiting for transfers between devices: 34.3 us -> 67.5 us  [from_chips(): lax.ppermute(lax.dynamic_slice_in_dim(a, (x + k) % 2 * w, w, 1), GROUP, [...]
    ppermute x1, waiting for transfers between devices: 2.28 us -> 14.4 us  [on_device(): about = lax.ppermute(about, GROUP, place(0))]
    ppermute x8 -> x4, starting transfers between devices: 18.9 us -> 7.74 us  [from_chips(): lax.ppermute(lax.dynamic_slice_in_dim(a, (x + k) % 2 * w, w, 1), GROUP, [...]
  transfers between devices with their start and end apart: 124 -> 72, of which waited for: 53 -> 33; matrix products, arithmetic and copies ran while one was open for 8% -> 11% of each run, Pallas kernels for 11% -> 16%
where the time goes in v2:
time: 607 us; the launch traced here: 598 us
  waiting for transfers between devices  296 us (49%)
  Pallas kernels  113 us (19%)
  starting transfers between devices  74.9 us (12%)
  local copies, waits for them, and re-layouts  55.7 us (9%)
  other arithmetic  42.4 us (7%)
  between operations  16.1 us (3%)
    ppermute x44, waiting for transfers between devices, swap2(): return lax.ppermute(a, axis, [(0, 1), (1, 0)])  108 us
    pallas_call x16, Pallas kernels, call(): pl.pallas_call(body, out_shape=tuple(outs), in_specs=[SM] + [VM] * len(ar...  93 us
    ppermute x4, waiting for transfers between devices, to_chips(): lax.ppermute(lax.dynamic_index_in_dim(halves, (z + k) % 2, 0, False), GRO...  79.6 us
    ppermute x4, waiting for transfers between devices, from_chips(): lax.ppermute(lax.dynamic_slice_in_dim(a, (x + k) % 2 * w, w, 1), GROUP, [...  67.5 us
    ppermute x44, starting transfers between devices, swap2(): return lax.ppermute(a, axis, [(0, 1), (1, 0)])  34.4 us
    unnamed x228, local copies, waits for them, and re-layouts  31.7 us
    ppermute x12, waiting for transfers between devices, shifted(): return lax.ppermute(a, axis, [(i, (i + s) % count) for i in range(count)])  26.3 us
    ppermute x12, starting transfers between devices, shifted(): return lax.ppermute(a, axis, [(i, (i + s) % count) for i in range(count)])  16.3 us
  transfers between devices with their start and end apart: 72, of which 33 were waited for; matrix products, arithmetic and copies ran while one was open for 11% of the time, Pallas kernels for 16%

profile of v2, /device:TPU:10, one launch (start us, length us, event | category | flops | bytes accessed | tf_op | source)
XLA Modules:
  0.0 597.6 jit_solution(4946735377010550993)
XLA Ops:
  23.3 5.7 ema_fwd.1
  35.7 39.1 %collective-permute-done.4.n0 = bf16[512,512]{1,0:T(8,128)(2,1)S(1)} collective-permute-done((bf16[512,512]{1,0:T(8,128)(2,1)}, bf16[512,512]{1,0:T(8,128)(2,1)S(1)}, u32[]{:S(2)}, u32[]{:S(2)}) %collective-permute-start.4) | collective-permute-done | bytes 524320 | tf_op jit(solution)/shard_map/ppermute | solution.py:543
  74.7 11.1 %collective-permute-done.5.n1 = bf16[512,512]{1,0:T(8,128)(2,1)S(1)} collective-permute-done((bf16[512,512]{1,0:T(8,128)(2,1)}, bf16[512,512]{1,0:T(8,128)(2,1)S(1)}, u32[]{:S(2)}, u32[]{:S(2)}) %collective-permute-start.5) | collective-permute-done | bytes 524320 | tf_op jit(solution)/shard_map/ppermute | solution.py:543
  90.6 16.7 %collective-permute-done.6.r1.v1 = bf16[3,2,256,256]{3,2,1,0:T(8,128)(2,1)} collective-permute-done((bf16[3,2,256,256]{3,2,1,0:T(8,128)(2,1)S(1)}, bf16[3,2,256,256]{3,2,1,0:T(8,128)(2,1)}, u32[]{:S(2)}, u32[]{:S(2)}) %collective-permute-start.6) | collective-permute-done | bytes 786464 | tf_op jit(solution)/shard_map/ppermute | solution.py:568
  114.0 14.4 %collective-permute-done.3 = f32[3,512]{0,1:T(8,128)S(1)} collective-permute-done((f32[3,512]{0,1:T(8,128)}, f32[3,512]{0,1:T(8,128)S(1)}, u32[]{:S(2)}, u32[]{:S(2)}) %collective-permute-start.3) | collective-permute-done | bytes 6176 | tf_op jit(solution)/shard_map/ppermute | solution.py:715
  133.9 5.6 value.1
  141.4 4.5 collective-permute-start.14
  147.7 23.7 %collective-permute-done.14 = bf16[512,256]{1,0:T(8,128)(2,1)} collective-permute-done((bf16[512,256]{1,0:T(8,128)(2,1)S(1)}, bf16[512,256]{1,0:T(8,128)(2,1)}, u32[]{:S(2)}, u32[]{:S(2)}) %collective-permute-start.14) | collective-permute-done | bytes 262176 | tf_op jit(solution)/shard_map/ppermute | solution.py:543
  171.4 5.6 collective-permute-done.15
  186.0 6.6 %collective-permute-done.19.g2 = bf16[512,512]{1,0:T(8,128)(2,1)} collective-permute-done((bf16[512,512]{1,0:T(8,128)(2,1)S(1)}, bf16[512,512]{1,0:T(8,128)(2,1)}, u32[]{:S(2)}, u32[]{:S(2)}) %collective-permute-start.19) | collective-permute-done | bytes 524320 | tf_op jit(solution)/shard_map/ppermute | solution.py:568
  195.3 5.7 collective-permute-done.13.r3
  203.1 7.0 %proj.1 = (bf16[512,1024]{1,0:T(8,128)(2,1)}, f32[512,1024]{1,0:T(8,128)}, f32[512,512]{1,0:T(8,128)}, f32[512,512]{1,0:T(8,128)}, f32[512,128]{1,0:T(8,128)S(1)...) custom-call(s32[6]{0:T(128)S(1)} %concatenate.107.idx, bf16[512,512]{1,0:T(8,128)(2,1)S(1)} %copy-done.29, ...), custom_call_target="tpu_custom_call" | custom-call | tf_op jit(solution)/shard_map/proj/pallas_call | solution.py:31
  210.4 4.7 collective-permute-done.17.vn
  217.8 8.3 %attend.1 = (bf16[512,1024]{1,0:T(8,128)(2,1)S(1)}, f32[512,1024]{1,0:T(8,128)}, bf16[512,1024]{1,0:T(8,128)(2,1)}, f32[512,512]{1,0:T(8,128)}, bf16[512,512]{1,0:T(8,128)(2,1)S(1)}) custom-call(s32[6]{0:T(128)S(1)} %concatenate.107.idx, bf16[512,128]{1,0:T(8,128)(2,1)S(1)} %get-tuple-element.116.qs, bf16[512,128]{1,0:T(8,128)(2,1)S(1)} %get-tuple-element.117.ko, ...), custom_call_target="tpu_custom_call" | custom-call | tf_op jit(solution)/shard_map/attend/pallas_call | solution.py:31
  243.1 12.9 %collective-permute-done.24.s2 = bf16[512,512]{1,0:T(8,128)(2,1)S(1)} collective-permute-done((bf16[512,512]{1,0:T(8,128)(2,1)S(1)}, bf16[512,512]{1,0:T(8,128)(2,1)S(1)}, u32[]{:S(2)}, u32[]{:S(2)}) %collective-permute-start.24) | collective-permute-done | bytes 524320 | tf_op jit(solution)/shard_map/ppermute | solution.py:568
  260.0 15.9 %collective-permute-done.27.o1 = bf16[3,256,512]{2,1,0:T(8,128)(2,1)S(1)} collective-permute-done((bf16[3,256,512]{2,1,0:T(8,128)(2,1)S(1)}, bf16[3,256,512]{2,1,0:T(8,128)(2,1)S(1)}, u32[]{:S(2)}, u32[]{:S(2)}) %collective-permute-start.27) | collective-permute-done | bytes 786464 | tf_op jit(solution)/shard_map/ppermute | solution.py:568
  276.8 12.6 %ffn.1 = (bf16[1024,1024]{1,0:T(8,128)(2,1)}, bf16[1024,1024]{1,0:T(8,128)(2,1)}, bf16[1024,1024]{1,0:T(8,128)(2,1)}, bf16[1024,1024]{1,0:T(8,128)(2,1)}, f32[51...) custom-call(s32[6]{0:T(128)S(1)} %concatenate.107.idx, bf16[512,512]{1,0:T(8,128)(2,1)S(1)} %unit.1.s0, ...), custom_call_target="tpu_custom_call" | custom-call | tf_op jit(solution)/shard_map/ffn/pallas_call | solution.py:31
  299.1 9.5 %grad_ffn.1 = (bf16[4,2,256,512]{3,2,1,0:T(8,128)(2,1)S(1)}, bf16[4,2,256,512]{3,2,1,0:T(8,128)(2,1)}) custom-call(s32[6]{0:T(128)S(1)} %concatenate.107.idx, bf16[1024,1024]{1,0:T(8,128)(2,1)} %get-tuple-element.133.low, bf16[1024,1024]{1,0:T(8,128)(2,1)} %get-tuple-element.138.gf, bf16[1024,1024]{1,0:T(8,128)(2,1)} %get-tuple-element.139.sf, ...), custom_call_target="tpu_custom_call" | custom-call | tf_op jit(solution)/shard_map/grad_ffn/pallas_call | solution.py:31
  316.6 4.2 grad_state.1
  326.2 8.4 %gate.1 = (bf16[512,1024]{1,0:T(8,128)(2,1)}, bf16[4,512,512]{2,1,0:T(8,128)(2,1)}, bf16[512,1024]{1,0:T(8,128)(2,1)}, bf16[512,1024]{1,0:T(8,128)(2,1)}) custom-call(s32[6]{0:T(128)S(1)} %concatenate.107.idx, bf16[512,512]{1,0:T(8,128)(2,1)} %get-tuple-element.149.h0, bf16[512,512]{1,0:T(8,128)(2,1)} %collective-permute-done.35.h1, ...), custom_call_target="tpu_custom_call" | custom-call | tf_op jit(solution)/shard_map/gate/pallas_call | solution.py:31
  335.9 5.4 attend_back.1
  355.4 5.6 grad_pack.1
  362.3 7.0 %collective-permute-done.37 = bf16[4,2,256,512]{3,2,1,0:T(8,128)(2,1)} collective-permute-done((bf16[4,2,256,512]{3,2,1,0:T(8,128)(2,1)}, bf16[4,2,256,512]{3,2,1,0:T(8,128)(2,1)}, u32[]{:S(2)}, u32[]{:S(2)}) %collective-permute-start.37) | collective-permute-done | bytes 2097184 | tf_op jit(solution)/shard_map/ppermute | solution.py:568
  370.8 16.9 %collective-permute-done.33 = bf16[512,512]{1,0:T(8,128)(2,1)S(1)} collective-permute-done((bf16[512,512]{1,0:T(8,128)(2,1)}, bf16[512,512]{1,0:T(8,128)(2,1)S(1)}, u32[]{:S(2)}, u32[]{:S(2)}) %collective-permute-start.33) | collective-permute-done | bytes 524320 | tf_op jit(solution)/shard_map/ppermute | solution.py:553
  392.7 12.1 %mixer_back.1 = (bf16[512,1024]{1,0:T(8,128)(2,1)}, bf16[512,128]{1,0:T(8,128)(2,1)}, f32[8,128]{1,0:T(8,128)}, f32[2,512,512]{2,1,0:T(8,128)}, bf16[2,512,512]{2,1,0:T(8,128)(2,1)}) custom-call(s32[6]{0:T(128)} %copy-done.70, f32[512,1024]{1,0:T(8,128)} %get-tuple-element.154.vown, bf16[512,1152]{1,0:T(8,128)(2,1)} %collective-permute-done.36.recv, ...), custom_call_target="tpu_custom_call" | custom-call | tf_op jit(solution)/shard_map/mixer_back/pallas_call | solution.py:31
  418.9 10.4 %collective-permute-done.49 = bf16[4,256,256]{2,1,0:T(8,128)(2,1)} collective-permute-done((bf16[4,256,256]{2,1,0:T(8,128)(2,1)}, bf16[4,256,256]{2,1,0:T(8,128)(2,1)}, u32[]{:S(2)}, u32[]{:S(2)}) %collective-permute-start.49) | collective-permute-done | bytes 524320 | tf_op jit(solution)/shard_map/ppermute | solution.py:568
  443.0 36.8 %collective-permute-done.39 = bf16[512,512]{1,0:T(8,128)(2,1)S(1)} collective-permute-done((bf16[512,512]{1,0:T(8,128)(2,1)S(1)}, bf16[512,512]{1,0:T(8,128)(2,1)S(1)}, u32[]{:S(2)}, u32[]{:S(2)}) %collective-permute-start.39) | collective-permute-done | bytes 524320 | tf_op jit(solution)/shard_map/ppermute | solution.py:553
  479.8 13.7 %collective-permute-done.40 = bf16[512,512]{1,0:T(8,128)(2,1)S(1)} collective-permute-done((bf16[512,512]{1,0:T(8,128)(2,1)S(1)}, bf16[512,512]{1,0:T(8,128)(2,1)S(1)}, u32[]{:S(2)}, u32[]{:S(2)}) %collective-permute-start.40) | collective-permute-done | bytes 524320 | tf_op jit(solution)/shard_map/ppermute | solution.py:553
  494.1 14.3 %ema_bwd.1 = (f32[1024,256]{1,0:T(8,128)S(1)}, f32[72,256]{1,0:T(8,128)S(1)}) custom-call(bf16[1024,256]{1,0:T(8,128)(2,1)S(1)} %slice.305.g_ref, f32[1024,256]{1,0:T(8,128)S(1)} %copy-done.37, f32[1024,256]{1,0:T(8,128)S(1)} %copy-done.5, f32[64,256]{1,0:T(8,128)S(1)} %pad_maximum_fusion.13.par_ref, f32[1,256]{1,0:T(1,128)S(1)} %bitcast.166, ...), custom_call_target="tpu_custom_call" | custom-call | tf_op jit(solution)/shard_map/ema_bwd/pallas_call | solution.py:210
  519.5 5.7 collective-permute-done.47
  540.5 6.6 %collective-permute-done.52 = bf16[256,512]{1,0:T(8,128)(2,1)} collective-permute-done((bf16[256,512]{1,0:T(8,128)(2,1)}, bf16[256,512]{1,0:T(8,128)(2,1)}, u32[]{:S(2)}, u32[]{:S(2)}) %collective-permute-start.52) | collective-permute-done | bytes 262176 | tf_op jit(solution)/shard_map/ppermute | solution.py:572
  547.1 17.0 %collective-permute-done.53 = bf16[256,512]{1,0:T(8,128)(2,1)} collective-permute-done((bf16[256,512]{1,0:T(8,128)(2,1)}, bf16[256,512]{1,0:T(8,128)(2,1)}, u32[]{:S(2)}, u32[]{:S(2)}) %collective-permute-start.53) | collective-permute-done | bytes 262176 | tf_op jit(solution)/shard_map/ppermute | solution.py:572
  (484 shorter events, 208.0 us)
Async XLA Ops:
  7.2 78.8 %all-gather.11.cloned.1.call-start = ((), (), s32[]{:S(2)}) async-start(), calls=%async_computation.6 | async-start | bytes 1310720 | tf_op jit(solution)/shard_map/all_gather | solution.py:694
  16.4 112.9 %all-gather.13.cloned.1.call-start = ((), (), s32[]{:S(2)}) async-start(), calls=%async_computation.7 | async-start | bytes 1638400 | tf_op jit(solution)/shard_map/all_gather | solution.py:694
  30.2 44.6 %collective-permute-start.4 = (bf16[512,512]{1,0:T(8,128)(2,1)}, bf16[512,512]{1,0:T(8,128)(2,1)S(1)}, u32[]{:S(2)}, u32[]{:S(2)}) collective-permute-start(bf16[512,512]{1,0:T(8,128)(2,1)} %get-tuple-element.281), channel_id=1, source_target_pairs={{0,0},{1,8},{2,4},{3,12},{4,1},{5,9},{6,5},{7,13},{8,2},{9,10},{10... | collective-permute-start | bytes 1572872 | tf_op jit(solution)/shard_map/ppermute | solution.py:543
  32.4 53.4 %collective-permute-start.5 = (bf16[512,512]{1,0:T(8,128)(2,1)}, bf16[512,512]{1,0:T(8,128)(2,1)S(1)}, u32[]{:S(2)}, u32[]{:S(2)}) collective-permute-start(bf16[512,512]{1,0:T(8,128)(2,1)} %get-tuple-element.280), channel_id=1, source_target_pairs={{0,8},{1,0},{2,12},{3,4},{4,9},{5,1},{6,13},{7,5},{8,10},{9,2},{10... | collective-permute-start | bytes 1572872 | tf_op jit(solution)/shard_map/ppermute | solution.py:543
  85.9 141.9 %all-gather.7.cloned.1.call-start = ((), (), s32[]{:S(2)}) async-start(), calls=%async_computation.2 | async-start | bytes 1310720 | tf_op jit(solution)/shard_map/all_gather | solution.py:694
  90.6 150.2 %all-gather.9.cloned.1.call-start = ((), (), s32[]{:S(2)}) async-start(), calls=%async_computation.3 | async-start | bytes 1310720 | tf_op jit(solution)/shard_map/all_gather | solution.py:694
  107.4 24.2 %collective-permute-start.10 = (bf16[3,2,256,256]{3,2,1,0:T(8,128)(2,1)}, bf16[3,2,256,256]{3,2,1,0:T(8,128)(2,1)S(1)}, u32[]{:S(2)}, u32[]{:S(2)}) collective-permute-start(bf16[3,2,256,256]{3,2,1,0:T(8,128)(2,1)} %collective-permute-done.6.r1.v1), channel_id=1, source_target_pairs={{0,16},{16,0},{1,17},{17,1},{2,18},{18,2},{3,19},{19,3},{4,20},{20... | collective-permute-start | bytes 2359304 | tf_op jit(solution)/shard_map/ppermute | solution.py:568
  139.7 38.7 %collective-permute-start.12 = (bf16[3,256,512]{2,1,0:T(8,128)(2,1)S(1)}, bf16[3,256,512]{2,1,0:T(8,128)(2,1)}, u32[]{:S(2)}, u32[]{:S(2)}) collective-permute-start(bf16[3,256,512]{2,1,0:T(8,128)(2,1)S(1)} %pad_maximum_fusion.4.r0), channel_id=1, source_target_pairs={{0,16},{16,0},{1,17},{17,1},{2,18},{18,2},{3,19},{19,3},{4,20},{20... | collective-permute-start | bytes 2359304 | tf_op jit(solution)/shard_map/ppermute | solution.py:568
  141.2 39.3 %collective-permute-start.11 = (bf16[3,256,512]{2,1,0:T(8,128)(2,1)S(1)}, bf16[3,256,512]{2,1,0:T(8,128)(2,1)}, u32[]{:S(2)}, u32[]{:S(2)}) collective-permute-start(bf16[3,256,512]{2,1,0:T(8,128)(2,1)S(1)} %pad_maximum_fusion.4.r0), channel_id=1, source_target_pairs={{0,8},{8,0},{1,9},{9,1},{2,10},{10,2},{3,11},{11,3},{4,12},{12,4},... | collective-permute-start | bytes 2359304 | tf_op jit(solution)/shard_map/ppermute | solution.py:568
  141.4 30.1 %collective-permute-start.14 = (bf16[512,256]{1,0:T(8,128)(2,1)S(1)}, bf16[512,256]{1,0:T(8,128)(2,1)}, u32[]{:S(2)}, u32[]{:S(2)}) collective-permute-start(bf16[512,256]{1,0:T(8,128)(2,1)S(1)} %get-tuple-element.288), channel_id=1, source_target_pairs={{0,0},{1,8},{2,4},{3,12},{4,1},{5,9},{6,5},{7,13},{8,2},{9,10},{10... | collective-permute-start | bytes 786440 | tf_op jit(solution)/shard_map/ppermute | solution.py:543
  145.8 31.2 %collective-permute-start.15 = (bf16[512,256]{1,0:T(8,128)(2,1)S(1)}, bf16[512,256]{1,0:T(8,128)(2,1)}, u32[]{:S(2)}, u32[]{:S(2)}) collective-permute-start(bf16[512,256]{1,0:T(8,128)(2,1)S(1)} %get-tuple-element.289), channel_id=1, source_target_pairs={{0,8},{1,0},{2,12},{3,4},{4,9},{5,1},{6,13},{7,5},{8,10},{9,2},{10... | collective-permute-start | bytes 786440 | tf_op jit(solution)/shard_map/ppermute | solution.py:543
  178.5 36.6 %collective-permute-start.17 = (bf16[512,1024]{1,0:T(8,128)(2,1)}, bf16[512,1024]{1,0:T(8,128)(2,1)}, u32[]{:S(2)}, u32[]{:S(2)}) collective-permute-start(bf16[512,1024]{1,0:T(8,128)(2,1)} %get-tuple-element.110.vo), channel_id=1, source_target_pairs={{0,8},{8,0},{1,9},{9,1},{2,10},{10,2},{3,11},{11,3},{4,12},{12,4},... | collective-permute-start | bytes 3145736 | tf_op jit(solution)/shard_map/ppermute | solution.py:568
  184.7 246.8 %reduce-scatter.3.cloned.1.call-start = ((), (), s32[]{:S(2)}) async-start(), calls=%async_computation.4 | async-start | bytes 348160 | tf_op jit(solution)/shard_map/reduce_scatter | solution.py:861
  184.9 25.4 %collective-permute-start.18 = (bf16[512,512]{1,0:T(8,128)(2,1)S(1)}, bf16[512,512]{1,0:T(8,128)(2,1)S(1)}, u32[]{:S(2)}, u32[]{:S(2)}) collective-permute-start(bf16[512,512]{1,0:T(8,128)(2,1)S(1)} %maximum_select_fusion.2.g0.cot), channel_id=1, source_target_pairs={{0,4},{4,0},{1,5},{5,1},{2,6},{6,2},{3,7},{7,3},{8,12},{12,8},{9,1... | collective-permute-start | bytes 1572872 | tf_op jit(solution)/shard_map/ppermute | solution.py:568
  242.5 33.4 %collective-permute-start.27 = (bf16[3,256,512]{2,1,0:T(8,128)(2,1)S(1)}, bf16[3,256,512]{2,1,0:T(8,128)(2,1)S(1)}, u32[]{:S(2)}, u32[]{:S(2)}) collective-permute-start(bf16[3,256,512]{2,1,0:T(8,128)(2,1)S(1)} %pad_maximum_fusion.6.o0), channel_id=1, source_target_pairs={{0,16},{16,0},{1,17},{17,1},{2,18},{18,2},{3,19},{19,3},{4,20},{20... | collective-permute-start | bytes 2359304 | tf_op jit(solution)/shard_map/ppermute | solution.py:568
  243.1 32.8 %collective-permute-start.23 = (bf16[512,512]{1,0:T(8,128)(2,1)S(1)}, bf16[512,512]{1,0:T(8,128)(2,1)S(1)}, u32[]{:S(2)}, u32[]{:S(2)}) collective-permute-start(bf16[512,512]{1,0:T(8,128)(2,1)S(1)} %unit.1.s0), channel_id=1, source_target_pairs={{0,4},{4,0},{1,5},{5,1},{2,6},{6,2},{3,7},{7,3},{8,12},{12,8},{9,1... | collective-permute-start | bytes 1572872 | tf_op jit(solution)/shard_map/ppermute | solution.py:568
  321.0 48.2 %collective-permute-start.37 = (bf16[4,2,256,512]{3,2,1,0:T(8,128)(2,1)}, bf16[4,2,256,512]{3,2,1,0:T(8,128)(2,1)}, u32[]{:S(2)}, u32[]{:S(2)}) collective-permute-start(bf16[4,2,256,512]{3,2,1,0:T(8,128)(2,1)} %get-tuple-element.164), channel_id=1, source_target_pairs={{0,16},{16,0},{1,17},{17,1},{2,18},{18,2},{3,19},{19,3},{4,20},{20... | collective-permute-start | bytes 6291464 | tf_op jit(solution)/shard_map/ppermute | solution.py:568
  342.4 50.3 %collective-permute-start.36 = (bf16[512,1152]{1,0:T(8,128)(2,1)}, bf16[512,1152]{1,0:T(8,128)(2,1)}, u32[]{:S(2)}, u32[]{:S(2)}) collective-permute-start(bf16[512,1152]{1,0:T(8,128)(2,1)} %pad_maximum_fusion), channel_id=1, source_target_pairs={{0,8},{8,0},{1,9},{9,1},{2,10},{10,2},{3,11},{11,3},{4,12},{12,4},... | collective-permute-start | bytes 3538952 | tf_op jit(solution)/shard_map/ppermute | solution.py:568
  346.9 40.8 %collective-permute-start.33 = (bf16[512,512]{1,0:T(8,128)(2,1)}, bf16[512,512]{1,0:T(8,128)(2,1)S(1)}, u32[]{:S(2)}, u32[]{:S(2)}) collective-permute-start(bf16[512,512]{1,0:T(8,128)(2,1)} %get-tuple-element.261), channel_id=1, source_target_pairs={{0,0},{8,1},{4,2},{12,3},{1,4},{9,5},{5,6},{13,7},{2,8},{10,9},{6,... | collective-permute-start | bytes 1572872 | tf_op jit(solution)/shard_map/ppermute | solution.py:553
  349.3 38.4 %collective-permute-start.34 = (bf16[512,512]{1,0:T(8,128)(2,1)}, bf16[512,512]{1,0:T(8,128)(2,1)S(1)}, u32[]{:S(2)}, u32[]{:S(2)}) collective-permute-start(bf16[512,512]{1,0:T(8,128)(2,1)} %get-tuple-element.262), channel_id=1, source_target_pairs={{8,0},{0,1},{12,2},{4,3},{9,4},{1,5},{13,6},{5,7},{10,8},{2,9},{14... | collective-permute-start | bytes 1572872 | tf_op jit(solution)/shard_map/ppermute | solution.py:553
  355.1 54.9 %collective-permute-start.42 = (bf16[2,4,256,256]{3,2,1,0:T(8,128)(2,1)}, bf16[2,4,256,256]{3,2,1,0:T(8,128)(2,1)}, u32[]{:S(2)}, u32[]{:S(2)}) collective-permute-start(bf16[2,4,256,256]{3,2,1,0:T(8,128)(2,1)} %get-tuple-element.177), channel_id=1, source_target_pairs={{0,8},{8,0},{1,9},{9,1},{2,10},{10,2},{3,11},{11,3},{4,12},{12,4},... | collective-permute-start | bytes 3145736 | tf_op jit(solution)/shard_map/ppermute | solution.py:568
  369.3 69.0 %collective-permute-start.41 = (bf16[2,4,256,512]{3,2,1,0:T(8,128)(2,1)}, bf16[2,4,256,512]{3,2,1,0:T(8,128)(2,1)}, u32[]{:S(2)}, u32[]{:S(2)}) collective-permute-start(bf16[2,4,256,512]{3,2,1,0:T(8,128)(2,1)} %get-tuple-element.176), channel_id=1, source_target_pairs={{0,16},{16,0},{1,17},{17,1},{2,18},{18,2},{3,19},{19,3},{4,20},{20... | collective-permute-start | bytes 6291464 | tf_op jit(solution)/shard_map/ppermute | solution.py:568
  410.0 158.6 %reduce-scatter.5.cloned.1.call-start = ((), (), s32[]{:S(2)}) async-start(), calls=%async_computation.5 | async-start | bytes 2621440 | tf_op jit(solution)/shard_map/reduce_scatter | solution.py:621
  416.4 96.6 %collective-permute-start.50 = (bf16[2,4,256,256]{3,2,1,0:T(8,128)(2,1)S(1)}, bf16[2,4,256,256]{3,2,1,0:T(8,128)(2,1)}, u32[]{:S(2)}, u32[]{:S(2)}) collective-permute-start(bf16[2,4,256,256]{3,2,1,0:T(8,128)(2,1)S(1)} %get-tuple-element.186), channel_id=1, source_target_pairs={{0,8},{8,0},{1,9},{9,1},{2,10},{10,2},{3,11},{11,3},{4,12},{12,4},... | collective-permute-start | bytes 3145736 | tf_op jit(solution)/shard_map/ppermute | solution.py:568
  434.9 44.9 %collective-permute-start.39 = (bf16[512,512]{1,0:T(8,128)(2,1)S(1)}, bf16[512,512]{1,0:T(8,128)(2,1)S(1)}, u32[]{:S(2)}, u32[]{:S(2)}) collective-permute-start(bf16[512,512]{1,0:T(8,128)(2,1)S(1)} %get-tuple-element.255), channel_id=1, source_target_pairs={{0,0},{8,1},{4,2},{12,3},{1,4},{9,5},{5,6},{13,7},{2,8},{10,9},{6,... | collective-permute-start | bytes 1572872 | tf_op jit(solution)/shard_map/ppermute | solution.py:553
  438.0 55.5 %collective-permute-start.40 = (bf16[512,512]{1,0:T(8,128)(2,1)S(1)}, bf16[512,512]{1,0:T(8,128)(2,1)S(1)}, u32[]{:S(2)}, u32[]{:S(2)}) collective-permute-start(bf16[512,512]{1,0:T(8,128)(2,1)S(1)} %get-tuple-element.256), channel_id=1, source_target_pairs={{8,0},{0,1},{12,2},{4,3},{9,4},{1,5},{13,6},{5,7},{10,8},{2,9},{14... | collective-permute-start | bytes 1572872 | tf_op jit(solution)/shard_map/ppermute | solution.py:553
  441.7 93.2 %collective-permute-start.56 = (bf16[4,256,512]{2,1,0:T(8,128)(2,1)}, bf16[4,256,512]{2,1,0:T(8,128)(2,1)}, u32[]{:S(2)}, u32[]{:S(2)}) collective-permute-start(bf16[4,256,512]{2,1,0:T(8,128)(2,1)} %slice_bitcast_fusion), channel_id=1, source_target_pairs={{0,8},{8,0},{1,9},{9,1},{2,10},{10,2},{3,11},{11,3},{4,12},{12,4},... | collective-permute-start | bytes 3145736 | tf_op jit(solution)/shard_map/ppermute | solution.py:568
  528.9 35.2 %collective-permute-start.53 = (bf16[256,512]{1,0:T(8,128)(2,1)}, bf16[256,512]{1,0:T(8,128)(2,1)}, u32[]{:S(2)}, u32[]{:S(2)}) collective-permute-start(bf16[256,512]{1,0:T(8,128)(2,1)} %get-tuple-element.253), channel_id=1, source_target_pairs={{0,2},{1,3},{2,0},{3,1},{4,6},{5,7},{6,4},{7,5},{8,10},{9,11},{10,... | collective-permute-start | bytes 786440 | tf_op jit(solution)/shard_map/ppermute | solution.py:572
  530.7 33.9 %collective-permute-start.54 = (bf16[256,512]{1,0:T(8,128)(2,1)}, bf16[256,512]{1,0:T(8,128)(2,1)}, u32[]{:S(2)}, u32[]{:S(2)}) collective-permute-start(bf16[256,512]{1,0:T(8,128)(2,1)} %get-tuple-element.254), channel_id=1, source_target_pairs={{0,3},{1,0},{2,1},{3,2},{4,7},{5,4},{6,5},{7,6},{8,11},{9,8},{10,9... | collective-permute-start | bytes 786440 | tf_op jit(solution)/shard_map/ppermute | solution.py:572
  536.6 36.7 %collective-permute-start.57 = (bf16[256,512]{1,0:T(8,128)(2,1)S(1)}, bf16[256,512]{1,0:T(8,128)(2,1)S(1)}, u32[]{:S(2)}, u32[]{:S(2)}) collective-permute-start(bf16[256,512]{1,0:T(8,128)(2,1)S(1)} %get-tuple-element.249), channel_id=1, source_target_pairs={{0,1},{1,2},{2,3},{3,0},{4,5},{5,6},{6,7},{7,4},{8,9},{9,10},{10,1... | collective-permute-start | bytes 786440 | tf_op jit(solution)/shard_map/ppermute | solution.py:572
  538.6 34.6 %collective-permute-start.58 = (bf16[256,512]{1,0:T(8,128)(2,1)S(1)}, bf16[256,512]{1,0:T(8,128)(2,1)S(1)}, u32[]{:S(2)}, u32[]{:S(2)}) collective-permute-start(bf16[256,512]{1,0:T(8,128)(2,1)S(1)} %get-tuple-element.251), channel_id=1, source_target_pairs={{0,2},{1,3},{2,0},{3,1},{4,6},{5,7},{6,4},{7,5},{8,10},{9,11},{10,... | collective-permute-start | bytes 786440 | tf_op jit(solution)/shard_map/ppermute | solution.py:572
  547.1 27.9 %collective-permute-start.59 = (bf16[256,512]{1,0:T(8,128)(2,1)S(1)}, bf16[256,512]{1,0:T(8,128)(2,1)}, u32[]{:S(2)}, u32[]{:S(2)}) collective-permute-start(bf16[256,512]{1,0:T(8,128)(2,1)S(1)} %get-tuple-element.250), channel_id=1, source_target_pairs={{0,3},{1,0},{2,1},{3,2},{4,7},{5,4},{6,5},{7,6},{8,11},{9,8},{10,9... | collective-permute-start | bytes 786440 | tf_op jit(solution)/shard_map/ppermute | solution.py:572
  (152 other events, 2443.2 us)
Sparse Core Ops, SparseCore 0:
  16.6 50.7 all-gather.10
  86.0 38.8 all-gather.12
  127.1 42.9 all-gather.6
  184.8 28.9 all-gather.8
  410.1 15.8 reduce-scatter.2
  428.1 62.8 reduce-scatter.4
